TPU v7x, 32 devices: a whole 2x2x4 slice. The times are simulated.
32 devices in a mesh: ctx: 8 (over y, x, core), wa: 4 (over z).
Axes of the slice: x: 2, y: 2, z: 4, core: 2. Of those that a mesh axis runs over, the one named last changes fastest.
Arguments:
- inputs: bfloat16 [4, 4096, 768], P('wa', 'ctx'), may hold values from -6 to 6
- cotangent: bfloat16 [4, 4096, 768], P('wa', 'ctx'), may hold values from -6 to 6
- lengths: int32 [4], P('wa'), may hold values from 2049 to 4096, as said below
- global_ids: int32 [4, 2], P('wa'), may hold values from 0 to 63, as said below
- random_ids: int32 [4, 64, 3], P('wa', 'ctx'), may hold values from 0 to 63, as said below
- attn_master: float32 [4, 768, 768], P(None, 'wa')
- attn_m: float32 [4, 768, 768], P(None, 'wa'), may hold values from -120 to 120
- attn_v: float32 [4, 768, 768], P(None, 'wa'), may hold values from 100 to 10000
- ffn_master: float32 [2, 768, 3072], P(None, 'wa')
- ffn_m: float32 [2, 768, 3072], P(None, 'wa'), may hold values from -120 to 120
- ffn_v: float32 [2, 768, 3072], P(None, 'wa'), may hold values from 100 to 10000
- vec_master: float32 [8, 768], P(None, 'wa')
- vec_m: float32 [8, 768], P(None, 'wa'), may hold values from -120 to 120
- vec_v: float32 [8, 768], P(None, 'wa'), may hold values from 100 to 10000
- bias_master: float32 [3072], P('wa'), may hold values from -3 to 3
- bias_m: float32 [3072], P('wa'), may hold values from -120 to 120
- bias_v: float32 [3072], P('wa'), may hold values from 100 to 10000
Outputs:
- output: bfloat16 [4, 4096, 768], P('wa', 'ctx')
- input_grad: float32 [4, 4096, 768], P('wa', 'ctx')
- attn_grad: float32 [4, 768, 768], P(None, 'wa')
- ffn_grad: float32 [2, 768, 3072], P(None, 'wa')
- vec_grad: float32 [8, 768], P(None, 'wa')
- bias_grad: float32 [3072], P('wa')
- attn_new: float32 [4, 768, 768], P(None, 'wa')
- ffn_new: float32 [2, 768, 3072], P(None, 'wa')
- vec_new: float32 [8, 768], P(None, 'wa')
- bias_new: float32 [3072], P('wa')
- attn_copy: bfloat16 [4, 768, 768], P(None, 'wa')
- ffn_copy: bfloat16 [2, 768, 3072], P(None, 'wa')
- vec_copy: bfloat16 [8, 768], P(None, 'wa')
- bias_copy: bfloat16 [3072], P('wa')
- attn_m_new: float32 [4, 768, 768], P(None, 'wa')
- ffn_m_new: float32 [2, 768, 3072], P(None, 'wa')
- vec_m_new: float32 [8, 768], P(None, 'wa')
- bias_m_new: float32 [3072], P('wa')
- attn_v_new: float32 [4, 768, 768], P(None, 'wa')
- ffn_v_new: float32 [2, 768, 3072], P(None, 'wa')
- vec_v_new: float32 [8, 768], P(None, 'wa')
- bias_v_new: float32 [3072], P('wa')
- norms: float32 [6, 2], replicated
- ratios: float32 [6], replicated
Inputs may be any that keep to these rules, and one draw needn't show every extreme that they name: `lengths`: every sequence uses more than half of its 4096 positions, and at least one uses all of them. `global_ids`: two different blocks of a sequence that lie wholly below its length. `random_ids`: blocks of the same sequence that lie wholly below its length; repeats may occur; of the 24 entries of the query blocks on one index of ctx, at most 6 name blocks held by any one index of ctx, and in every sequence the first index of ctx has exactly 6 entries naming blocks of the first.
All inputs are finite; a program needn't handle non-finite values.
Results may differ from a plain program's by a relative error of at most 0.025.
Values may be sent and summed in bfloat16 or wider, within the bound.
No kernel may reach another device: no remote copies, remote signals or barrier semaphores. Data moves between devices by JAX's collectives and lax.ppermute only.
A program may use at most 384 MiB of HBM per device.

v0:
```python
import functools

import jax
import jax.numpy as jnp
from jax import lax
from jax.experimental import pallas as pl
from jax.experimental.pallas import tpu as pltpu
from jax.sharding import PartitionSpec as P


D = 768
HEADS = 12
HEAD = 64
FF = 3072
BLOCK = 64
RAND = 3
SLOTS = 8
PAIRS = HEADS // 2
PAIR = 2 * HEAD
QUADS = HEADS // 4
QUAD = 4 * HEAD

MASKED_SCORE = -1e30
LN_EPS = 1e-06
ADAM_EPS = 1e-06
RATIO_EPS = 1e-06
BETA_ONE = 0.5
BETA_TWO = 0.5
WEIGHT_DECAY = 0.01
STEP_RATE = 0.2

CTX = "ctx"
WA = "wa"

F32 = jnp.float32
BF16 = jnp.bfloat16
NT = (((1,), (1,)), ((), ()))
NN = (((1,), (0,)), ((), ()))
TN = (((0,), (0,)), ((), ()))


def mm(a, b, dims=NN):
    return lax.dot_general(a, b, dims, preferred_element_type=F32)


def heads_apart(part):
    lane = lax.broadcasted_iota(jnp.int32, part.shape, 1) // HEAD
    zero = jnp.zeros_like(part)
    return jnp.concatenate(
        [jnp.where(lane == head, part, zero) for head in range(part.shape[1] // HEAD)], axis=0
    )


def heads_joined(parts):
    count = parts.shape[1] // HEAD
    rows = parts.shape[0] // count
    lane = lax.broadcasted_iota(jnp.int32, (rows, parts.shape[1]), 1) // HEAD
    joined = parts[:rows]
    for head in range(1, count):
        joined = jnp.where(lane == head, parts[head * rows : (head + 1) * rows], joined)
    return joined


FRINGE = 4


def window_places(i, blocks):
    before = jnp.where(i == 0, blocks, i - 1)
    after = jnp.where(i == blocks - 1, blocks + 1, i + 1)
    return before, i, after


def slot_scores(keys, queries, nvalid_ref, base):
    s = mm(keys, queries, NT)
    row = lax.broadcasted_iota(jnp.int32, (BLOCK, s.shape[1]), 0)
    parts = [
        jnp.where(row < nvalid_ref[base + at], s[at * BLOCK : (at + 1) * BLOCK], MASKED_SCORE)
        for at in range(3)
    ]
    return jnp.concatenate(parts + [s[3 * BLOCK :]], axis=0)


def slot_rows(near_ref, rand_ref, i, columns):
    blocks = near_ref.shape[0] - FRINGE
    places = window_places(i, blocks) + (blocks + 2, blocks + 3)
    rows = [near_ref[at, :, columns] for at in places]
    return jnp.concatenate(rows + [rand_ref[at, :, columns] for at in range(RAND)], axis=0)


def sparse_fwd_kernel(nvalid_ref, q_ref, near_ref, rand_ref, out_ref, lse_ref):
    i = pl.program_id(0)
    for h in range(QUADS):
        cols = slice(h * QUAD, (h + 1) * QUAD)
        vcols = slice(D + h * QUAD, D + (h + 1) * QUAD)
        queries = heads_apart(q_ref[:, cols])
        k = slot_rows(near_ref, rand_ref, i, cols)
        v = slot_rows(near_ref, rand_ref, i, vcols)
        s = slot_scores(k, queries, nvalid_ref, i * 3)
        top = jnp.max(s, axis=0, keepdims=True)
        p = jnp.exp(s - top)
        total = jnp.sum(p, axis=0, keepdims=True)
        p = (p * (1.0 / total)).astype(BF16)
        out_ref[:, cols] = heads_joined(mm(p, v, TN)).astype(BF16)
        lse_ref[0, h : h + 1, :] = top + jnp.log(total)


def sparse_bwd_kernel(
    nvalid_ref, q_ref, do_ref, lse_ref, near_ref, rand_ref, dq_ref, grads_ref, acc_ref
):
    i = pl.program_id(0)

    @pl.when(i == 0)
    def _():
        acc_ref[...] = jnp.zeros_like(acc_ref)

    blocks = near_ref.shape[0] - FRINGE
    places = window_places(i, blocks) + (blocks + 2, blocks + 3)
    for h in range(QUADS):
        cols = slice(h * QUAD, (h + 1) * QUAD)
        vcols = slice(D + h * QUAD, D + (h + 1) * QUAD)
        queries = heads_apart(q_ref[:, cols])
        douts = heads_apart(do_ref[:, cols])
        k = slot_rows(near_ref, rand_ref, i, cols)
        v = slot_rows(near_ref, rand_ref, i, vcols)
        s = slot_scores(k, queries, nvalid_ref, i * 3)
        p = jnp.exp(s - lse_ref[0, h : h + 1, :])
        dp = mm(v, douts, NT)
        ds = (p * (dp - jnp.sum(p * dp, axis=0, keepdims=True))).astype(BF16)
        dq = heads_joined(mm(ds, k, TN)) * (HEAD**-0.5)
        dq_ref[:, cols] = dq.astype(BF16)
        dk = mm(ds, queries).reshape(SLOTS, BLOCK, QUAD)
        dv = mm(p.astype(BF16), douts).reshape(SLOTS, BLOCK, QUAD)
        for grad, to in ((dk, cols), (dv, vcols)):
            for at, place in enumerate(places):
                acc_ref[place, :, to] += grad[at]
            grads_ref[:, :, to] = grad[len(places) :].astype(BF16)


def piece_copies(held, slot, buf_ref, sems, to):
    group, place = divmod(slot, GROUP)
    side, place = divmod(place, 4)
    own, first, second, up, low = held[10 * group + 5 * side : 10 * group + 5 * side + 5]
    half = buf_ref.shape[1] // 2
    if place < 3:
        return [pltpu.make_async_copy((own, first, second)[place], buf_ref.at[to], sems.at[to, 0])]
    return [
        pltpu.make_async_copy(up, buf_ref.at[to, pl.ds(0, half)], sems.at[to, 0]),
        pltpu.make_async_copy(low, buf_ref.at[to, pl.ds(half, half)], sems.at[to, 1]),
    ]


def global_fwd_kernel(pair_ref, nvalid_ref, q_ref, k_ref, v_ref, b_ref, *refs):
    held = refs[:-6]
    out_ref, top_ref, sum_ref, acc_ref, buf_ref, sems = refs[-6:]
    c = pl.program_id(0)
    rows = q_ref.shape[0]
    keys = buf_ref.shape[1]
    count = len(held) // 10 * GROUP

    @pl.when(c == 0)
    def _():
        top_ref[...] = jnp.full_like(top_ref, MASKED_SCORE)
        sum_ref[...] = jnp.zeros_like(sum_ref)
        acc_ref[...] = jnp.zeros_like(acc_ref)

    for at in range(count):

        @pl.when(c == at)
        def _():
            if at == 0:
                for copy in piece_copies(held, 0, buf_ref, sems, 0):
                    copy.start()
            if at + 1 < count:
                for copy in piece_copies(held, at + 1, buf_ref, sems, (at + 1) % 2):
                    copy.start()
            for copy in piece_copies(held, at, buf_ref, sems, at % 2):
                copy.wait()

    @pl.when(nvalid_ref[c] > 0)
    def _():
        x = buf_ref[lax.rem(c, 2)]
        k = mm(x, k_ref[...]).astype(BF16)
        v = (mm(x, v_ref[...]) + b_ref[...]).astype(BF16)
        ok = lax.broadcasted_iota(jnp.int32, (keys, 2 * rows), 0) < nvalid_ref[c]
        s = jnp.where(ok, mm(k, heads_apart(q_ref[...]), NT), MASKED_SCORE)
        before = top_ref[...]
        top = jnp.maximum(before, jnp.max(s, axis=0, keepdims=True))
        p = jnp.exp(s - top)
        shrink = jnp.exp(before - top)
        sum_ref[...] = sum_ref[...] * shrink + jnp.sum(p, axis=0, keepdims=True)
        acc_ref[...] = acc_ref[...] * shrink + mm(v, p.astype(BF16), TN)
        top_ref[...] = top

    @pl.when(c == pl.num_programs(0) - 1)
    def _():
        total = sum_ref[...]
        lse = top_ref[...] + jnp.log(total)
        out_ref[:rows] = heads_joined((acc_ref[...] / total).T)
        out_ref[rows : rows + 1] = lse[:, :rows]
        out_ref[rows + 1 : rows + 2] = lse[:, rows:]
        out_ref[rows + 2 :] = jnp.zeros((6, PAIR), F32)


def global_bwd_kernel(
    nvalid_ref, q_ref, do_ref, out_ref, kv_ref, near_ref, used_ref, own_ref, dq_ref, res_ref
):
    rows = q_ref.shape[0]
    keys = kv_ref.shape[0]
    ok = lax.broadcasted_iota(jnp.int32, (keys, 2 * rows), 0) < nvalid_ref[0]
    dq_ref[:rows] = jnp.zeros((rows, D), BF16)
    for h in range(PAIRS):
        cols = slice(h * PAIR, (h + 1) * PAIR)
        vcols = slice(D + h * PAIR, D + (h + 1) * PAIR)
        queries = heads_apart(q_ref[:, cols])
        douts = heads_apart(do_ref[:, cols])
        outs = jnp.concatenate([out_ref[h, :rows], out_ref[h, :rows]], axis=0)
        dot = jnp.sum((douts.astype(F32) * outs).T, axis=0, keepdims=True)
        lse = jnp.concatenate(
            [out_ref[h, rows : rows + 1], out_ref[h, rows + 1 : rows + 2]], axis=1
        )
        k = kv_ref[:, cols]
        v = kv_ref[:, vcols]
        p = jnp.where(ok, jnp.exp(mm(k, queries, NT) - lse), 0.0)
        ds = (p * (mm(v, douts, NT) - dot)).astype(BF16)
        dq = heads_joined(mm(ds, k, TN)) * (HEAD**-0.5)
        dq_ref[rows:, cols] = dq.astype(BF16)
        for grad, at in ((mm(ds, queries), cols), (mm(p.astype(BF16), douts), vcols)):
            res_ref[:keys, at] = (near_ref[:keys, at] + grad).astype(BF16)
            res_ref[keys:, at] = near_ref[keys:, at].astype(BF16)


def kv_used_kernel(source_ref, index_ref, w_ref, b_ref, *refs):
    held = refs[:-4]
    kv_ref, x_ref, buf_ref, sems = refs[-4:]
    step = pl.program_id(0)
    count = buf_ref.shape[1] // BLOCK

    def rows_of(to, at):
        return buf_ref.at[to, pl.ds(at * BLOCK, BLOCK)]

    def fetch(group, to):
        for at in range(count):
            place = group * count + at
            for which, ref in enumerate(held):

                @pl.when(source_ref[place] == which)
                def _():
                    start = pl.multiple_of(index_ref[place] * BLOCK, BLOCK)
                    pltpu.make_async_copy(
                        ref.at[pl.ds(start, BLOCK)], rows_of(to, at), sems.at[to, at]
                    ).start()

    now = lax.rem(step, 2)

    @pl.when(step == 0)
    def _():
        fetch(0, 0)

    @pl.when(step + 1 < pl.num_programs(0))
    def _():
        fetch(step + 1, 1 - now)

    for at in range(count):
        pltpu.make_async_copy(
            held[0].at[pl.ds(0, BLOCK)], rows_of(now, at), sems.at[now, at]
        ).wait()
    rows = buf_ref[now]
    x_ref[...] = rows
    kv_ref[...] = (mm(rows, w_ref[...]) + b_ref[...]).astype(BF16)


def place_blocks_kernel(table_ref, x_ref, q_ref, low_ref, high_ref):
    low_ref[...] = jnp.zeros_like(low_ref)
    high_ref[...] = jnp.zeros_like(high_ref)
    limit = low_ref.shape[0]

    def step(s, with_query):
        to = table_ref[s]
        part = x_ref[s] + q_ref[s] if with_query else x_ref[s]

        @pl.when(to < limit)
        def _():
            low_ref[to] += part

        @pl.when(to >= limit)
        def _():
            high_ref[to - limit] += part

    @pl.loop(0, q_ref.shape[0])
    def _(s):
        step(s, True)

    @pl.loop(q_ref.shape[0], x_ref.shape[0])
    def _(s):
        step(s, False)


def whole(shape):
    return pl.BlockSpec(shape, lambda *a: (0,) * len(shape))


VMEM_SPEC = pl.BlockSpec(memory_space=pltpu.VMEM)
SMEM_SPEC = pl.BlockSpec(memory_space=pltpu.SMEM)


def cost(flops, moved, exps=0):
    return pl.CostEstimate(flops=int(flops), bytes_accessed=int(moved), transcendentals=int(exps))


def near_spec(near):
    return pl.BlockSpec((near, BLOCK, 2 * D), lambda i, n: (0, 0, 0))


def rand_spec(near):
    return pl.BlockSpec((RAND, BLOCK, 2 * D), lambda i, n: (near // RAND + i, 0, 0))


def sparse_fwd(nvalid, q, kv_used):
    rows = q.shape[0]
    blocks = rows // BLOCK
    near = blocks + FRINGE
    work = 2 * rows * SLOTS * BLOCK * D
    return pl.pallas_call(
        sparse_fwd_kernel,
        grid_spec=pltpu.PrefetchScalarGridSpec(
            num_scalar_prefetch=1,
            grid=(blocks,),
            in_specs=[
                pl.BlockSpec((BLOCK, D), lambda i, n: (i, 0)),
                near_spec(near),
                rand_spec(near),
            ],
            out_specs=[
                pl.BlockSpec((BLOCK, D), lambda i, n: (i, 0)),
                pl.BlockSpec((1, 8, QUAD), lambda i, n: (i, 0, 0)),
            ],
        ),
        out_shape=[
            jax.ShapeDtypeStruct((rows, D), BF16),
            jax.ShapeDtypeStruct((blocks, 8, QUAD), F32),
        ],
        cost_estimate=cost(2 * work, rows * SLOTS * D * 4, rows * SLOTS * BLOCK * HEADS),
        name="sf",
    )(nvalid, q, kv_used, kv_used)


def sparse_bwd(nvalid, q, dout, lse, kv_used):
    rows = q.shape[0]
    blocks = rows // BLOCK
    near = blocks + FRINGE
    used = kv_used.shape[0]
    work = 2 * rows * SLOTS * BLOCK * D
    return pl.pallas_call(
        sparse_bwd_kernel,
        grid_spec=pltpu.PrefetchScalarGridSpec(
            num_scalar_prefetch=1,
            grid=(blocks,),
            in_specs=[
                pl.BlockSpec((BLOCK, D), lambda i, n: (i, 0)),
                pl.BlockSpec((BLOCK, D), lambda i, n: (i, 0)),
                pl.BlockSpec((1, 8, QUAD), lambda i, n: (i, 0, 0)),
                near_spec(near),
                rand_spec(near),
            ],
            out_specs=[
                pl.BlockSpec((BLOCK, D), lambda i, n: (i, 0)),
                rand_spec(near),
                near_spec(near),
            ],
        ),
        out_shape=[
            jax.ShapeDtypeStruct((near * BLOCK, D), BF16),
            jax.ShapeDtypeStruct((used, BLOCK, 2 * D), BF16),
            jax.ShapeDtypeStruct((near, BLOCK, 2 * D), F32),
        ],
        cost_estimate=cost(5 * work, rows * SLOTS * D * 8, rows * SLOTS * BLOCK * HEADS),
        name="sb",
    )(nvalid, q, dout, lse, kv_used, kv_used)


def global_fwd(pair, nvalid, q, w_kv, kv_bias, held):
    rows = q.shape[0]
    chunks = nvalid.shape[0]
    keys = held[0].shape[0]
    return pl.pallas_call(
        global_fwd_kernel,
        grid_spec=pltpu.PrefetchScalarGridSpec(
            num_scalar_prefetch=2,
            grid=(chunks,),
            in_specs=[
                pl.BlockSpec((rows, PAIR), lambda c, p, n: (0, p[0])),
                pl.BlockSpec((D, PAIR), lambda c, p, n: (0, p[0])),
                pl.BlockSpec((D, PAIR), lambda c, p, n: (0, PAIRS + p[0])),
                pl.BlockSpec((1, PAIR), lambda c, p, n: (0, PAIRS + p[0])),
            ]
            + [pl.BlockSpec(memory_space=pl.ANY)] * len(held),
            out_specs=pl.BlockSpec((rows + 8, PAIR), lambda c, p, n: (0, 0)),
            scratch_shapes=[pltpu.VMEM((1, 2 * rows), F32)] * 2
            + [
                pltpu.VMEM((PAIR, 2 * rows), F32),
                pltpu.VMEM((2, keys, D), BF16),
                pltpu.SemaphoreType.DMA((2, 2)),
            ],
        ),
        out_shape=jax.ShapeDtypeStruct((rows + 8, PAIR), F32),
        cost_estimate=cost(
            4 * (rows + D) * chunks * keys * PAIR,
            2 * chunks * keys * D,
            2 * rows * chunks * keys,
        ),
        name="gf",
    )(pair[None], nvalid, q, w_kv, w_kv, kv_bias, *held)


def global_bwd(nvalid, q, dout, out, kv_used, near, used, dq):
    rows = q.shape[0]
    near_rows = near.shape[0] * BLOCK
    keys = near_rows - FRINGE * BLOCK
    near = near.reshape(near_rows, 2 * D)
    used_rows = used.shape[0] * BLOCK
    fringe = FRINGE * BLOCK
    return pl.pallas_call(
        global_bwd_kernel,
        grid_spec=pltpu.PrefetchScalarGridSpec(
            num_scalar_prefetch=1,
            grid=(1,),
            in_specs=[
                whole((rows, D)),
                whole((rows, D)),
                whole(out.shape),
                whole((keys, 2 * D)),
                whole((near_rows, 2 * D)),
                pl.BlockSpec(memory_space=pl.ANY),
                pl.BlockSpec(memory_space=pl.ANY),
            ],
            out_specs=[
                pl.BlockSpec((fringe, D), lambda i, n: (keys // fringe, 0)),
                whole((near_rows, 2 * D)),
            ],
        ),
        out_shape=[
            jax.ShapeDtypeStruct((near_rows, D), BF16),
            jax.ShapeDtypeStruct((used_rows, 2 * D), BF16),
        ],
        input_output_aliases={6: 1, 7: 0},
        cost_estimate=cost(10 * rows * keys * D, near_rows * D * 12, rows * keys * HEADS),
        name="gb",
    )(
        nvalid,
        q,
        dout,
        out,
        kv_used.reshape(used_rows, 2 * D),
        near,
        used.reshape(used_rows, 2 * D),
        dq,
    )


def kv_used_rows(source, index, w_kv, kv_bias, held):
    count = source.shape[0]
    each = 4
    rows = each * BLOCK
    return pl.pallas_call(
        kv_used_kernel,
        grid_spec=pltpu.PrefetchScalarGridSpec(
            num_scalar_prefetch=2,
            grid=(count // each,),
            in_specs=[whole((D, 2 * D)), whole((1, 2 * D))]
            + [pl.BlockSpec(memory_space=pl.ANY)] * len(held),
            out_specs=[
                pl.BlockSpec((rows, 2 * D), lambda t, *a: (t, 0)),
                pl.BlockSpec((rows, D), lambda t, *a: (t, 0)),
            ],
            scratch_shapes=[
                pltpu.VMEM((2, rows, D), BF16),
                pltpu.SemaphoreType.DMA((2, each)),
            ],
        ),
        out_shape=[
            jax.ShapeDtypeStruct((count * BLOCK, 2 * D), BF16),
            jax.ShapeDtypeStruct((count * BLOCK, D), BF16),
        ],
        cost_estimate=cost(4 * count * BLOCK * D * D, 8 * count * BLOCK * D),
        name="kv",
    )(source, index, w_kv, kv_bias, *held)


def place_blocks(table, x_blocks, q_blocks, total):
    half = jax.ShapeDtypeStruct((total // 2,) + x_blocks.shape[1:], BF16)
    return pl.pallas_call(
        place_blocks_kernel,
        in_specs=[SMEM_SPEC, VMEM_SPEC, VMEM_SPEC],
        out_specs=[VMEM_SPEC, VMEM_SPEC],
        out_shape=[half, half],
        cost_estimate=cost(0, 2 * (total + 2 * x_blocks.shape[0]) * BLOCK * D),
        name="pb",
    )(table, x_blocks, q_blocks)


CORE, FIRST, SECOND = 1, 2, 4
GROUP = 8
CUT = 3 * D // GROUP + D // GROUP


def exchange(value, mask):
    count = lax.axis_size(CTX)
    return lax.ppermute(value, CTX, [(i, i ^ mask) for i in range(count)])


def slot_of(index):
    return index // GROUP * GROUP + index // 2 % 4 + index % 2 * 4


def index_of(slot):
    return slot // GROUP * GROUP + slot % 4 * 2 + slot // 4 % 2


def spare_masks():
    return [1 << i for i in range(3, lax.axis_size(CTX).bit_length() - 1)]


def all_masks():
    return [CORE, FIRST, SECOND] + spare_masks()


def wa_shift(value, step):
    count = lax.axis_size(WA)
    return lax.ppermute(value, WA, [(i, (i + step) % count) for i in range(count)])


def wa_parts(piece):
    return [piece] + [wa_shift(piece, step) for step in range(1, lax.axis_size(WA))]


def wa_reduce(chunks):
    count = lax.axis_size(WA)
    rank = lax.axis_index(WA)

    def chunk(step):
        return lax.dynamic_index_in_dim(chunks, (rank + step) % count, 0, keepdims=False)

    arrived = [wa_shift(chunk(step), step) for step in range(1, count)]
    total = chunk(0).astype(F32)
    for part in arrived:
        total = total + part.astype(F32)
    return total


def wa_total(value):
    count = lax.axis_size(WA)
    rank = lax.axis_index(WA)
    parts = jnp.stack(wa_parts(value))
    total = parts[rank % count]
    for index in range(1, count):
        total = total + parts[(rank - index) % count]
    return total


def bit_of(mask):
    return (lax.axis_index(CTX) // mask) % 2 == 1


def gather_group(own, then=None):
    cut = own.shape[0] // 2
    first = exchange(own, FIRST)
    second = exchange(own, SECOND)
    upper, lower = first[:cut], second[cut:]
    if then is not None:
        upper, lower, then = lax.optimization_barrier((upper, lower, then))
    upper = exchange(upper, SECOND)
    lower = exchange(lower, FIRST)
    near = [own, first, second, upper, lower]
    held = near + [exchange(part, CORE) for part in near]
    return held if then is None else (held, then)


def group_in_order(own):
    value = own[None]
    for mask in (FIRST, SECOND, CORE):
        other = exchange(value, mask)
        high = bit_of(mask)
        value = jnp.concatenate(
            [jnp.where(high, other, value), jnp.where(high, value, other)], axis=0
        )
    return value


def add_low(first, second):
    return (first.astype(F32) + second.astype(F32)).astype(BF16)


def cut_kernel(where_ref, attn_ref, ffn_ref, vec_ref, bias_ref, attn_out, ffn_out):
    wide = attn_ref.shape[1]
    attn_out[:wide, :] = attn_ref[0].astype(BF16)
    small = jnp.concatenate([vec_ref[...], bias_ref[...], jnp.zeros((4, wide), F32)], axis=0)
    attn_out[wide:, :wide] = small.astype(BF16)
    attn_out[wide:, wide:] = jnp.zeros((16, CUT - wide), BF16)
    ffn_out[:, :CUT] = ffn_ref[0].astype(BF16)
    ffn_out[:, CUT:] = ffn_ref[1].astype(BF16)


def cut_pieces(slot, attn_master, ffn_master, vec_master, bias_rows):
    wide = attn_master.shape[1]
    return pl.pallas_call(
        cut_kernel,
        grid_spec=pltpu.PrefetchScalarGridSpec(
            num_scalar_prefetch=1,
            grid=(1,),
            in_specs=[
                pl.BlockSpec((1, wide, CUT), lambda i, w: (w[0] // 2, 0, w[0] % 2)),
                pl.BlockSpec((2, wide, CUT), lambda i, w: (0, 0, w[0])),
                whole((8, wide)),
                whole((4, wide)),
            ],
            out_specs=[whole((wide + 16, CUT)), whole((wide, 2 * CUT))],
        ),
        out_shape=[
            jax.ShapeDtypeStruct((wide + 16, CUT), BF16),
            jax.ShapeDtypeStruct((wide, 2 * CUT), BF16),
        ],
        cost_estimate=cost(0, wide * CUT * 18),
        name="cut",
    )(slot[None], attn_master, ffn_master, vec_master, bias_rows)


def join_kernel(rank_ref, *refs):
    parts, outs = refs[: len(refs) - 2], refs[len(refs) - 2 :]
    count = len(parts)
    wide = outs[0].shape[0] // count
    for step, part in enumerate(parts):
        at = lax.rem(rank_ref[0] - step + count, count)
        outs[0][pl.ds(pl.multiple_of(at * wide, 16), wide), :] = part[:wide]
        outs[1][at] = part[part.shape[0] - 16 :]


def join_rows(rank, parts):
    count = len(parts)
    extra = parts[0].shape[0] % 32
    wide = parts[0].shape[0] - extra
    columns = parts[0].shape[1]
    return pl.pallas_call(
        join_kernel,
        in_specs=[SMEM_SPEC] + [VMEM_SPEC] * count,
        out_specs=[VMEM_SPEC, VMEM_SPEC],
        out_shape=[
            jax.ShapeDtypeStruct((count * wide, columns), BF16),
            jax.ShapeDtypeStruct((count, 16, columns), BF16),
        ],
        cost_estimate=cost(0, 4 * count * wide * columns),
        name="join",
    )(rank[None], *parts)


def held_specs(rows, columns, tiles):
    shape = (rows // tiles, columns)
    middle = tiles // 2
    each = [
        pl.BlockSpec(shape, lambda t, *a: (t, 0)),
        pl.BlockSpec(shape, lambda t, *a: (t, 0)),
        pl.BlockSpec(shape, lambda t, *a: (t, 0)),
        pl.BlockSpec(shape, lambda t, *a: (jnp.minimum(t, middle - 1), 0)),
        pl.BlockSpec(shape, lambda t, *a: (jnp.maximum(t - middle, 0), 0)),
    ]
    return each + each


def for_each_slot(held, body):
    upper = pl.program_id(0) < pl.num_programs(0) // 2
    for side in range(2):
        own, first, second, up, low = held[5 * side : 5 * side + 5]
        for at, ref in enumerate((own, first, second)):
            body(4 * side + at, ref)
        pl.when(upper)(functools.partial(body, 4 * side + 3, up))
        pl.when(jnp.logical_not(upper))(functools.partial(body, 4 * side + 3, low))


def attn_weights_kernel(slot_ref, *refs):
    held, (q_ref, kv_ref, o_ref) = refs[:10], refs[10:]

    def body(slot, ref):
        at = slot_ref[0] ^ slot
        for out, start, stop in ((q_ref, 0, 2), (kv_ref, 2, 6), (o_ref, 6, 8)):

            @pl.when((at >= start) & (at < stop))
            def _():
                out[:, pl.ds(pl.multiple_of((at - start) * CUT, 128), CUT)] = ref[...]

    for_each_slot(held, body)


def attn_weights(slot, held):
    rows = held[0].shape[0]
    tiles = 4
    size = rows // tiles
    widths = (D, 2 * D, D)
    return pl.pallas_call(
        attn_weights_kernel,
        grid_spec=pltpu.PrefetchScalarGridSpec(
            num_scalar_prefetch=1,
            grid=(tiles,),
            in_specs=held_specs(rows, CUT, tiles),
            out_specs=[pl.BlockSpec((size, w), lambda t, *a: (t, 0)) for w in widths],
        ),
        out_shape=[jax.ShapeDtypeStruct((rows, w), BF16) for w in widths],
        cost_estimate=cost(0, 4 * rows * GROUP * CUT),
        name="aw",
    )(slot[None], *held)


STRIDE = 2


def matrix_copies(held, step, up_ref, down_ref, sems, to):
    jobs = []
    for at in range(STRIDE):
        side, place = divmod(step * STRIDE + at, 4)
        own, first, second, upper, lower = held[5 * side : 5 * side + 5]
        half = D // 2
        parts = [((own, first, second)[place], 0, D)] if place < 3 else [(upper, 0, half), (lower, half, half)]
        for ref, start, size in parts:
            for which, buf in enumerate((up_ref, down_ref)):
                source = ref.at[:, pl.ds(which * CUT, CUT)]
                target = buf.at[to, pl.ds(start, size), pl.ds(at * CUT, CUT)]
                jobs.append(pltpu.make_async_copy(source, target, sems.at[to, len(jobs)]))
    return jobs


def fetch_matrices(held, up_ref, down_ref, sems):
    step = pl.program_id(0)
    for at in range(GROUP // STRIDE):

        @pl.when(step == at)
        def _():
            if at == 0:
                for copy in matrix_copies(held, 0, up_ref, down_ref, sems, 0):
                    copy.start()
            if at + 1 < GROUP // STRIDE:
                for copy in matrix_copies(held, at + 1, up_ref, down_ref, sems, (at + 1) % 2):
                    copy.start()
            for copy in matrix_copies(held, at, up_ref, down_ref, sems, at % 2):
                copy.wait()

    return lax.rem(step, 2)


def add_up(total_ref, part):
    @pl.when(pl.program_id(0) == 0)
    def _():
        total_ref[...] = part

    @pl.when(pl.program_id(0) > 0)
    def _():
        total_ref[...] += part


def ffn_fwd_kernel(n_ref, b_ref, *refs):
    held = refs[:10]
    hidden_ref, slope_ref, total_ref, w_up_ref, w_down_ref, up_ref, down_ref, sems = refs[10:]
    now = fetch_matrices(held, up_ref, down_ref, sems)
    up = mm(n_ref[...], up_ref[now]) + b_ref[0]
    cdf = 0.5 * (1.0 + lax.erf(up * (0.5**0.5)))
    hidden = (up * cdf).astype(BF16)
    hidden_ref[...] = hidden
    slope_ref[...] = (cdf + up * (jnp.exp(-0.5 * up * up) * 0.3989422804014327)).astype(BF16)
    add_up(total_ref, mm(hidden, down_ref[now], NT))
    w_up_ref[...] = up_ref[now]
    w_down_ref[...] = down_ref[now]


def ffn_scratch():
    buf = pltpu.VMEM((2, D, STRIDE * CUT), BF16)
    return [buf, buf, pltpu.SemaphoreType.DMA((2, 4 * STRIDE))]


def ffn_fwd(norm_low, bias, held):
    rows = norm_low.shape[0]
    wide = pl.BlockSpec((rows, STRIDE * CUT), lambda t: (0, t))
    full = pl.BlockSpec((D, STRIDE * CUT), lambda t: (0, t))
    return pl.pallas_call(
        ffn_fwd_kernel,
        grid=(GROUP // STRIDE,),
        in_specs=[whole((rows, D)), pl.BlockSpec((1, 1, STRIDE * CUT), lambda t: (t, 0, 0))]
        + [pl.BlockSpec(memory_space=pl.ANY)] * 10,
        out_specs=[wide, wide, whole((rows, D)), full, full],
        out_shape=[
            jax.ShapeDtypeStruct((rows, FF), BF16),
            jax.ShapeDtypeStruct((rows, FF), BF16),
            jax.ShapeDtypeStruct((rows, D), F32),
            jax.ShapeDtypeStruct((D, FF), BF16),
            jax.ShapeDtypeStruct((D, FF), BF16),
        ],
        scratch_shapes=ffn_scratch(),
        cost_estimate=cost(4 * rows * D * FF, 4 * rows * FF + 4 * D * FF, 2 * rows * FF),
        name="ff",
    )(norm_low, bias.reshape(-1, 1, STRIDE * CUT), *held)


def spread_kernel(slot_ref, *refs, read):
    keep = refs[: len(refs) - 5]
    x_ref, y_ref, own_ref, first_ref, second_ref = refs[len(refs) - 5 :]
    upper = pl.program_id(0) < pl.num_programs(0) // 2

    def part(slot):
        return read(slot_ref, keep, slot).astype(BF16)

    own_ref[...] = part(0)

    @pl.when(upper)
    def _():
        x_ref[0] = part(3)
        x_ref[1] = part(1)
        second_ref[...] = part(2)

    @pl.when(jnp.logical_not(upper))
    def _():
        y_ref[0] = part(3)
        y_ref[1] = part(2)
        first_ref[...] = part(1)


def read_ffn(slot_ref, refs, slot):
    at = slice(slot * CUT, (slot + 1) * CUT)
    up, down, up_in, down_in = (r[:, at].astype(F32) for r in refs)
    return jnp.concatenate([up + up_in, down + down_in], axis=1)


def read_attn(slot_ref, refs, slot):
    at = (slot_ref[0] ^ slot) % 4
    columns = pl.ds(pl.multiple_of(at % 2 * CUT, 128), CUT)
    return refs[0][at // 2, :, columns].astype(F32) + refs[1][at // 2, :, columns].astype(F32)


def read_rows(slot_ref, refs, slot):
    return refs[0][slot].astype(F32) + refs[1][slot].astype(F32)


def spread(slot, arrays, in_specs, rows, columns, read, tiles):
    size = rows // tiles
    middle = tiles // 2
    low = lambda t: jnp.minimum(t, middle - 1)
    high = lambda t: jnp.maximum(t - middle, 0)
    half = jax.ShapeDtypeStruct((rows // 2, columns), BF16)
    pair = jax.ShapeDtypeStruct((2, rows // 2, columns), BF16)
    return pl.pallas_call(
        functools.partial(spread_kernel, read=read),
        grid_spec=pltpu.PrefetchScalarGridSpec(
            num_scalar_prefetch=1,
            grid=(tiles,),
            in_specs=in_specs,
            out_specs=[
                pl.BlockSpec((2, size, columns), lambda t, *a: (0, low(t), 0)),
                pl.BlockSpec((2, size, columns), lambda t, *a: (0, high(t), 0)),
                pl.BlockSpec((size, columns), lambda t, *a: (t, 0)),
                pl.BlockSpec((size, columns), lambda t, *a: (high(t), 0)),
                pl.BlockSpec((size, columns), lambda t, *a: (low(t), 0)),
            ],
        ),
        out_shape=[pair, pair, jax.ShapeDtypeStruct((rows, columns), BF16), half, half],
        cost_estimate=cost(0, rows * columns * 24),
    )(slot[None], *arrays)


def reduce_group(slot, arrays, in_specs, rows, columns, read, tiles=4):
    x_out, y_out, own, first, second = spread(slot, arrays, in_specs, rows, columns, read, tiles)
    x_in = exchange(x_out, FIRST)
    y_in = exchange(y_out, SECOND)
    x_last = exchange(add_low(first, y_in[0]), FIRST)
    y_last = exchange(add_low(second, x_in[0]), SECOND)
    cut = rows // 2
    upper = own[:cut].astype(F32) + x_in[1].astype(F32) + y_last.astype(F32)
    lower = own[cut:].astype(F32) + y_in[1].astype(F32) + x_last.astype(F32)
    return upper, lower


def adam_kernel(slot_ref, *refs, pieces):
    held = refs[:10]
    w_ref, m_ref, v_ref, grad_ref, first_ref, second_ref, step_ref, sums_ref = refs[10:]

    def body(slot, ref):
        at = slot_ref[0] ^ slot
        if pieces == 1:
            columns = pl.ds(pl.multiple_of(at % 2 * CUT, 128), CUT)
            grad_ref[at // 2, :, columns] = ref[...].astype(F32)
        else:
            columns = pl.ds(pl.multiple_of(at * CUT, 128), CUT)
            grad_ref[0, :, columns] = ref[:, :CUT].astype(F32)
            grad_ref[1, :, columns] = ref[:, CUT:].astype(F32)

    for_each_slot(held, body)

    @pl.when(pl.program_id(0) == 0)
    def _():
        sums_ref[...] = jnp.zeros_like(sums_ref)

    mats, rows, columns = grad_ref.shape
    each = 8 if columns > D else 24

    @pl.loop(0, mats * (rows // each))
    def _(step):
        mat = step // (rows // each)
        here = pl.ds(pl.multiple_of(step % (rows // each) * each, each), each)
        grad = grad_ref[mat, here]
        first = BETA_ONE * m_ref[mat, here] + (1.0 - BETA_ONE) * grad
        second = BETA_TWO * v_ref[mat, here] + (1.0 - BETA_TWO) * grad * grad
        weight = w_ref[mat, here]
        move = first / (jnp.sqrt(second) + ADAM_EPS) + WEIGHT_DECAY * weight
        first_ref[mat, here] = first
        second_ref[mat, here] = second
        step_ref[mat, here] = move
        for row, part in ((mat, weight), (mats + mat, move)):
            sums_ref[row] += jnp.sum((part * part).reshape(each // 8, 8, columns), axis=0)


def final(ratios, master, step):
    new = master - (STEP_RATE * ratios)[:, None, None] * step
    return new, new.astype(BF16)


def adam(slot, held, master, first, second):
    mats, wide, columns = master.shape
    tiles = 2
    size = wide // tiles
    piece_columns = held[0].shape[1]
    block = pl.BlockSpec((mats, size, columns), lambda t, *a: (0, t, 0))
    full = jax.ShapeDtypeStruct(master.shape, F32)
    return pl.pallas_call(
        functools.partial(adam_kernel, pieces=piece_columns // CUT),
        grid_spec=pltpu.PrefetchScalarGridSpec(
            num_scalar_prefetch=1,
            grid=(tiles,),
            in_specs=held_specs(wide, piece_columns, tiles) + [block] * 3,
            out_specs=[block] * 4 + [whole((2 * mats, 8, columns))],
        ),
        out_shape=[full] * 4 + [jax.ShapeDtypeStruct((2 * mats, 8, columns), F32)],
        cost_estimate=cost(20 * master.size, 30 * master.size, master.size),
    )(slot[None], *held, master, first, second)


def norm_parts(hidden):
    centre = hidden - jnp.mean(hidden, axis=-1, keepdims=True)
    spread = jnp.mean(centre * centre, axis=-1, keepdims=True)
    inverse = lax.rsqrt(spread + LN_EPS)
    return centre * inverse, inverse


def norm_back(grad, normal, inverse, gain):
    scaled = grad * gain
    return inverse * (
        scaled
        - jnp.mean(scaled, axis=-1, keepdims=True)
        - normal * jnp.mean(scaled * normal, axis=-1, keepdims=True)
    )


def adam_moments(first, second, grads):
    first_new = BETA_ONE * first + (1.0 - BETA_ONE) * grads
    second_new = BETA_TWO * second + (1.0 - BETA_TWO) * grads * grads
    return (first_new, second_new, first_new / (jnp.sqrt(second_new) + ADAM_EPS))


def shards(
    inputs,
    cotangent,
    lengths,
    global_ids,
    random_ids,
    attn_master,
    attn_m,
    attn_v,
    ffn_master,
    ffn_m,
    ffn_v,
    vec_master,
    vec_m,
    vec_v,
    bias_master,
    bias_m,
    bias_v,
):
    x = inputs[0]
    rows = x.shape[0]
    ctx_count = lax.axis_size(CTX)
    rank = lax.axis_index(CTX)
    wa_count = lax.axis_size(WA)
    wa_rank = lax.axis_index(WA)
    blocks = rows // BLOCK
    total_blocks = blocks * ctx_count
    wide = D // wa_count
    seq_len = lengths[0]
    glob_ids = global_ids[0]
    my_slot = slot_of(rank) % GROUP
    relative = jnp.arange(ctx_count, dtype=jnp.int32)
    owner_at = rank ^ index_of(relative)

    attn_piece, ffn_piece = cut_pieces(
        my_slot, attn_master, ffn_master, vec_master, bias_master.reshape(4, wide)
    )
    attn_parts = wa_parts(attn_piece)
    x_held, attn_parts = gather_group(x, attn_parts)
    attn_rows, small = join_rows(wa_rank, attn_parts)
    attn_held = gather_group(attn_rows)
    w_query, w_kv, w_out = attn_weights(my_slot, attn_held)
    ffn_parts = wa_parts(ffn_piece)
    ffn_parts, w_kv = lax.optimization_barrier((ffn_parts, w_kv))
    ffn_rows, _ = join_rows(wa_rank, ffn_parts)
    ffn_held = gather_group(ffn_rows)

    small = small[:, :, :wide]
    vectors = small[:, :8].transpose(1, 0, 2).reshape(8, D).astype(F32)
    bias_blocks = small[:, 8:12].reshape(GROUP, CUT).astype(F32)
    bias_up = bias_blocks[my_slot ^ relative[:GROUP]]

    def place_of(block):
        block = jnp.clip(block, 0, total_blocks - 1)
        return slot_of((block // blocks) ^ rank) * blocks + block % blocks

    rand_ids = random_ids[0]
    own_blocks = rank * blocks + jnp.arange(blocks, dtype=jnp.int32)
    window = jnp.stack([own_blocks - 1, own_blocks, own_blocks + 1], axis=1)
    window_nvalid = jnp.where(
        (window >= 0) & (window < total_blocks), jnp.clip(seq_len - window * BLOCK, 0, BLOCK), 0
    ).reshape(-1)
    used_table = place_of(
        jnp.concatenate(
            [own_blocks, own_blocks[:1] - 1, own_blocks[-1:] + 1, glob_ids, rand_ids.reshape(-1)]
        )
    )
    used_slot, used_at = used_table // blocks, used_table % blocks
    split = (used_slot % 4 == 3) & (used_at >= blocks // 2)
    used_source = used_slot // 4 * 5 + used_slot % 4 + split
    used_index = used_at - jnp.where(split, blocks // 2, 0)
    chunk_nvalid = jnp.clip(seq_len - owner_at * rows, 0, rows)
    positions = rank * rows + jnp.arange(rows, dtype=jnp.int32)
    row_weight = (positions < seq_len).astype(F32)[:, None]
    hits = own_blocks[None, :] == glob_ids[:, None]

    scale = HEAD**-0.5
    kv_bias = jnp.concatenate([jnp.zeros((D,), F32), vectors[1]])[None]
    groups = [x_held]
    for mask in spare_masks():
        groups += [[exchange(part, mask) for part in held] for held in groups]
    x_held = [part for held in groups for part in held]
    kv_used, x_used = kv_used_rows(used_source, used_index, w_kv, kv_bias, x_held)
    near_rows = (blocks + FRINGE) * BLOCK
    x_near = x_used[:near_rows]
    x_glob = x_near[near_rows - 2 * BLOCK :]
    kv_used = kv_used.reshape(-1, BLOCK, 2 * D)
    glob_query = ((mm(x_glob, w_query) + vectors[0]).astype(BF16) * BF16(scale)).astype(BF16)
    glob_part = global_fwd(
        jnp.minimum(my_slot, PAIRS - 1), chunk_nvalid, glob_query, w_kv, kv_bias, x_held
    )
    glob_pairs = group_in_order(glob_part)
    query = ((mm(x, w_query, NN) + vectors[0]).astype(BF16) * BF16(scale)).astype(BF16)
    sparse_out, lse = sparse_fwd(window_nvalid, query, kv_used)
    glob_out = (
        glob_pairs[:PAIRS, : 2 * BLOCK].transpose(1, 0, 2).reshape(2, BLOCK, D).astype(BF16)
    )
    attended = sparse_out.reshape(blocks, BLOCK, D)
    for g in range(2):
        attended = jnp.where(hits[g][:, None, None], glob_out[g][None], attended)
    attended = attended.reshape(rows, D)

    first_sum = x.astype(F32) + mm(attended, w_out) + vectors[2]
    normal_one, inverse_one = norm_parts(first_sum)
    norm_one = normal_one * vectors[4] + vectors[5]
    norm_low = norm_one.astype(BF16)
    hidden_low, slope, down, w_up, w_down = ffn_fwd(norm_low, bias_up, ffn_held)
    second_sum = norm_one + down + vectors[3]
    normal_two, inverse_two = norm_parts(second_sum)
    output = ((normal_two * vectors[6] + vectors[7]) * row_weight).astype(BF16)
    grad_out = cotangent[0].astype(F32) * row_weight
    grad_second = norm_back(grad_out, normal_two, inverse_two, vectors[6])
    grad_down = grad_second.astype(BF16)
    grad_upper = (mm(grad_down, w_down) * slope.astype(F32)).astype(BF16)
    grad_norm = grad_second + mm(grad_upper, w_up, NT)
    grad_first = norm_back(grad_norm, normal_one, inverse_one, vectors[4])
    grad_branch = grad_first.astype(BF16)
    grad_attended = mm(grad_branch, w_out, NT).astype(BF16)

    cut = FF // 2
    up_sent = mm(norm_low, grad_upper[:, cut:], TN).astype(BF16)
    down_sent = mm(grad_down, hidden_low[:, cut:], TN).astype(BF16)
    up_keep = mm(norm_low, grad_upper[:, :cut], TN).astype(BF16)
    down_keep = mm(grad_down, hidden_low[:, :cut], TN).astype(BF16)
    tiles = 4
    ffn_spec = pl.BlockSpec((D // tiles, cut), lambda t, *a: (t, 0))

    def finish(upper, lower):
        total = jnp.concatenate([upper, lower], axis=0).astype(BF16)
        for mask in spare_masks():
            total = add_low(total, exchange(total, mask))
        return wa_reduce(total.reshape(wa_count, wide, total.shape[1])).astype(BF16)

    ffn_mine = finish(
        *reduce_group(
            my_slot,
            [up_keep, down_keep, exchange(up_sent, CORE), exchange(down_sent, CORE)],
            [ffn_spec] * 4,
            D,
            2 * CUT,
            read_ffn,
            tiles,
        ),
    )
    ffn_grad, ffn_first, ffn_second, ffn_step, ffn_sums = adam(
        my_slot, gather_group(ffn_mine), ffn_master, ffn_m, ffn_v
    )

    grad_blocks = grad_attended.reshape(blocks, BLOCK, D)
    glob_part = jnp.sum(
        jnp.where(hits[:, :, None, None], grad_blocks[None], 0), axis=1, dtype=F32
    ).astype(BF16)
    for mask in all_masks():
        glob_part = glob_part + exchange(glob_part, mask)
    grad_glob = glob_part.reshape(2 * BLOCK, D)
    grad_sparse = jnp.where((hits[0] | hits[1])[:, None, None], 0, grad_blocks).reshape(rows, D)
    near_dquery, used_grads, near = sparse_bwd(window_nvalid, query, grad_sparse, lse, kv_used)
    near_dquery, used_grads = global_bwd(
        chunk_nvalid[:1], glob_query, grad_glob, glob_pairs, kv_used, near, used_grads, near_dquery
    )

    g_query = mm(x_near, near_dquery, TN).astype(BF16)
    g_kv = mm(x_used, used_grads, TN).astype(BF16)
    g_key, g_value = g_kv[:, :D], g_kv[:, D:]
    g_out = mm(attended, grad_branch, TN).astype(BF16)
    on_core = bit_of(CORE)
    early, late = jnp.stack([g_query, g_key]), jnp.stack([g_value, g_out])
    attn_sent = jnp.where(on_core, early, late)
    attn_keep = jnp.where(on_core, late, early)
    attn_spec = pl.BlockSpec((2, D // tiles, D), lambda t, *a: (0, t, 0))
    attn_mine = finish(
        *reduce_group(
            my_slot,
            [attn_keep, exchange(attn_sent, CORE)],
            [attn_spec] * 2,
            D,
            CUT,
            read_attn,
            tiles,
        ),
    )
    attn_grad, attn_first, attn_second, attn_step, attn_sums = adam(
        my_slot, gather_group(attn_mine), attn_master, attn_m, attn_v
    )

    dx_used = mm(used_grads, w_kv, NT).astype(BF16)
    dx_query = mm(near_dquery, w_query, NT).astype(BF16)
    dx_keep, dx_sent = place_blocks(
        used_table,
        dx_used.reshape(-1, BLOCK, D),
        dx_query.reshape(-1, BLOCK, D),
        total_blocks,
    )
    for mask in spare_masks()[::-1]:
        dx_keep = add_low(dx_keep, exchange(dx_sent, mask))
        dx_keep, dx_sent = jnp.split(dx_keep, 2, axis=0)
    dx_spec = pl.BlockSpec((4, rows // tiles, D), lambda t, *a: (0, t, 0))
    dx_own = reduce_group(
        my_slot,
        [dx_keep.reshape(4, rows, D), exchange(dx_sent, CORE).reshape(4, rows, D)],
        [dx_spec] * 2,
        rows,
        D,
        read_rows,
        tiles,
    )
    input_grad = grad_first + jnp.concatenate(dx_own, axis=0)

    vec_local = jnp.stack(
        [
            jnp.sum(near_dquery, axis=0, dtype=F32),
            jnp.sum(used_grads[:, D:], axis=0, dtype=F32),
            jnp.sum(grad_branch, axis=0, dtype=F32),
            jnp.sum(grad_down, axis=0, dtype=F32),
            jnp.sum(grad_norm * normal_one, axis=0),
            jnp.sum(grad_norm, axis=0),
            jnp.sum(grad_out * normal_two, axis=0),
            jnp.sum(grad_out, axis=0),
        ]
    )
    bias_local = jnp.sum(grad_upper, axis=0, dtype=F32).reshape(GROUP, CUT)[
        my_slot ^ relative[:GROUP]
    ]
    small_local = jnp.concatenate(
        [
            vec_local.reshape(8, wa_count, wide).transpose(1, 0, 2).reshape(wa_count, 8 * wide),
            bias_local.reshape(wa_count, FF // wa_count),
        ],
        axis=1,
    )
    small_sum = wa_reduce(small_local)
    for mask in all_masks():
        small_sum = small_sum + exchange(small_sum, mask)
    vec_grad = small_sum[: 8 * wide].reshape(8, wide)
    bias_grad = small_sum[8 * wide :]

    vec_first, vec_second, vec_adam = adam_moments(vec_m, vec_v, vec_grad)
    bias_first, bias_second, bias_adam = adam_moments(bias_m, bias_v, bias_grad)

    def ratio_of(sums):
        squares = jnp.sqrt(wa_total(jnp.sum(sums, axis=(1, 2))))
        count = squares.shape[0] // 2
        return squares[:count], squares[count:], squares[:count] / (squares[count:] + RATIO_EPS)

    ffn_norm, ffn_length, ffn_ratio = ratio_of(ffn_sums)
    ffn_new, ffn_copy = final(ffn_ratio, ffn_master, ffn_step)
    attn_norm, attn_length, attn_ratio = ratio_of(attn_sums)
    attn_new, attn_copy = final(attn_ratio, attn_master, attn_step)
    ratios = jnp.concatenate([attn_ratio, ffn_ratio])
    norms = jnp.stack(
        [
            jnp.concatenate([attn_norm, ffn_norm]),
            jnp.concatenate([attn_length, ffn_length]),
        ],
        axis=1,
    )
    vec_new = vec_master - STEP_RATE * vec_adam
    bias_new = bias_master - STEP_RATE * bias_adam
    return (
        output[None],
        input_grad[None],
        attn_grad,
        ffn_grad,
        vec_grad,
        bias_grad,
        attn_new,
        ffn_new,
        vec_new,
        bias_new,
        attn_copy,
        ffn_copy,
        vec_new.astype(BF16),
        bias_new.astype(BF16),
        attn_first,
        ffn_first,
        vec_first,
        bias_first,
        attn_second,
        ffn_second,
        vec_second,
        bias_second,
        norms,
        ratios,
    )


def solution(mesh):
    tokens = P(WA, CTX, None)
    mats = P(None, WA, None)
    vecs = P(None, WA)
    line = P(WA)
    state = (mats, mats, vecs, line)
    in_specs = (
        (tokens, tokens, P(WA), P(WA, None), tokens)
        + (mats,) * 6
        + (vecs,) * 3
        + (line,) * 3
    )
    out_specs = (tokens, tokens) + state * 5 + (P(), P())
    return jax.shard_map(shards, mesh=mesh, in_specs=in_specs, out_specs=out_specs, check_vma=False)
```

profile of v0, /device:TPU:0, one launch (start us, length us, event | category | flops | bytes accessed | tf_op | source)
XLA Modules:
  0.0 508.7 jit_solution(14878581285454867810)
XLA Ops:
  0.7 3.1 collective-permute-start.4
  8.5 3.6 collective-permute-start.7
  13.1 8.4 %collective-permute-done.4.refs_2_ = bf16[512,768]{1,0:T(8,128)(2,1)S(1)} collective-permute-done((bf16[512,768]{1,0:T(8,128)(2,1)}, bf16[512,768]{1,0:T(8,128)(2,1)S(1)}, u32[]{:S(2)}, u32[]{:S(2)}) %collective-permute-start.4) | collective-permute-done | bytes 786464 | tf_op jit(solution)/shard_map/ppermute | solution.py:508
  21.5 3.8 collective-permute-start.2
  35.5 8.7 %collective-permute-done.9.refs_2_ = bf16[768,384]{1,0:T(8,128)(2,1)S(1)} collective-permute-done((bf16[768,384]{1,0:T(8,128)(2,1)}, bf16[768,384]{1,0:T(8,128)(2,1)S(1)}, u32[]{:S(2)}, u32[]{:S(2)}) %collective-permute-start.9) | collective-permute-done | bytes 589856 | tf_op jit(solution)/shard_map/ppermute | solution.py:508
  47.4 3.2 collective-permute-done.1.refs_2_
  57.1 3.4 collective-permute-done.11.refs_4_
  78.1 5.6 %aw.1 = (bf16[768,768]{1,0:T(8,128)(2,1)}, bf16[768,1536]{1,0:T(8,128)(2,1)}, bf16[768,768]{1,0:T(8,128)(2,1)}) custom-call(s32[1]{0:T(128)} %bitcast.5.where_ref.slot_ref, bf16[768,384]{1,0:T(8,128)(2,1)} %get-tuple-element.90.refs_0_, bf16[768,384]{1,0:T(8,128)(2,1)} %copy-done.10, bf16[768,384]{1,0:T(8,128)(2,1)} %copy-done.9, ...), custom_call_target="tpu_custom_call" | custom-call | bytes 9437184 | tf_op jit(solution)/shard_map/aw/pallas_call | solution.py:697
  83.8 14.3 %kv.1 = (bf16[2304,1536]{1,0:T(8,128)(2,1)}, bf16[2304,768]{1,0:T(8,128)(2,1)}) custom-call(s32[36]{0:T(128)} %convert_add_fusion.14.source_ref, s32[36]{0:T(128)} %get-tuple-element.187.index_ref, bf16[768,1536]{1,0:T(8,128)(2,1)} %get-tuple-element.92.w_ref.k_ref.v_ref, f32[1,1536]{1,0:T(1,128)} %broadcast_in_dim.142.b_ref, bf16[512,768]{1,0:T(8,128)(2,1)} %bitcast.232, ...), custom_call_target="tpu_custom_call" | custom-call | flops 5435817984 | bytes 14155776 | tf_op jit(solution)/shard_map/kv/pallas_call | solution.py:464
  100.1 11.1 %gf.1 = f32[136,128]{1,0:T(8,128)} custom-call(s32[1]{0:T(128)} %bitcast.3.pair_ref, s32[8]{0:T(128)} %fusion.66.nvalid_ref, bf16[128,768]{1,0:T(8,128)(2,1)} %fusion.28.q_ref, bf16[768,1536]{1,0:T(8,128)(2,1)} %get-tuple-element.92.w_ref.k_ref.v_ref, bf16[768,1536]{1,0:T(8,128)(2,1)} %get-tuple-element.92.w_ref.k_ref.v_ref, ...), custom_call_target="tpu_custom_call" | custom-call | flops 1879048192 | bytes 6291456 | tf_op jit(solution)/shard_map/gf/pallas_call | solution.py:385
  113.7 3.0 collective-permute-done.24
  128.2 14.8 %sf.1 = (bf16[512,768]{1,0:T(8,128)(2,1)}, f32[8,8,256]{2,1,0:T(8,128)}) custom-call(s32[24]{0:T(128)} %select_n.312.nvalid_ref, bf16[512,768]{1,0:T(8,128)(2,1)} %fusion.19.q_ref, bf16[36,64,1536]{2,1,0:T(8,128)(2,1)} %bitcast.213, bf16[36,64,1536]{2,1,0:T(8,128)(2,1)} %bitcast.214), custom_call_target="tpu_custom_call" | custom-call | flops 805306368 | bytes 12582912 | tf_op jit(solution)/shard_map/sf/pallas_call | solution.py:323
  144.4 7.6 %collective-permute-done.28.refs_2_ = bf16[768,768]{1,0:T(8,128)(2,1)} collective-permute-done((bf16[768,768]{1,0:T(8,128)(2,1)}, bf16[768,768]{1,0:T(8,128)(2,1)}, u32[]{:S(2)}, u32[]{:S(2)}) %collective-permute-start.28) | collective-permute-done | bytes 1179680 | tf_op jit(solution)/shard_map/ppermute | solution.py:508
  159.1 9.0 %collective-permute-done.30.refs_4_ = bf16[384,768]{1,0:T(8,128)(2,1)S(1)} collective-permute-done((bf16[384,768]{1,0:T(8,128)(2,1)S(1)}, bf16[384,768]{1,0:T(8,128)(2,1)S(1)}, u32[]{:S(2)}, u32[]{:S(2)}) %collective-permute-start.30) | collective-permute-done | bytes 589856 | tf_op jit(solution)/shard_map/ppermute | solution.py:508
  174.8 14.7 %ff.1 = (bf16[512,3072]{1,0:T(8,128)(2,1)}, bf16[512,3072]{1,0:T(8,128)(2,1)}, f32[512,768]{1,0:T(8,128)}, bf16[768,3072]{1,0:T(8,128)(2,1)}, bf16[768,3072]{1,0:T(8,128)(2,1)}) custom-call(bf16[512,768]{1,0:T(8,128)(2,1)} %fusion.17.n_ref, f32[4,1,768]{2,1,0:T(1,128)} %reshape.341.b_ref, bf16[768,768]{1,0:T(8,128)(2,1)} %get-tuple-element.105.refs_0_, ...), custom_call_target="tpu_custom_call" | custom-call | flops 4831838208 | bytes 15728640 | tf_op jit(solution)/shard_map/ff/pallas_call | solution.py:780
  195.3 3.1 convert_reduce_fusion.1
  198.5 2.8 convolution_convert_fusion.3
  201.3 2.8 convolution_convert_fusion.5.refs_0_
  204.2 3.4 multiply_reduce_fusion
  211.4 2.8 convolution_convert_fusion.2
  214.8 2.8 convolution_convert_fusion.4.refs_1_
  217.7 3.6 collective-permute-done.37
  225.3 23.0 %sb.1 = (bf16[768,768]{1,0:T(8,128)(2,1)}, bf16[36,64,1536]{2,1,0:T(8,128)(2,1)}, f32[12,64,1536]{2,1,0:T(8,128)}) custom-call(s32[24]{0:T(128)} %select_n.312.nvalid_ref, bf16[512,768]{1,0:T(8,128)(2,1)} %fusion.19.q_ref, bf16[512,768]{1,0:T(8,128)(2,1)} %get-tuple-element.227.do_ref, f32[8,8,256]{2,1,0:T(8,128)} %get-tuple-element.110.lse_ref, ...), custom_call_target="tpu_custom_call" | custom-call | flops 2013265920 | bytes 25165824 | tf_op jit(solution)/shard_map/sb/pallas_call | solution.py:353
  249.1 8.5 %gb.1 = (bf16[768,768]{1,0:T(8,128)(2,1)}, bf16[2304,1536]{1,0:T(8,128)(2,1)}) custom-call(s32[1]{0:T(128)} %bitcast.237, bf16[128,768]{1,0:T(8,128)(2,1)} %fusion.28.q_ref, bf16[128,768]{1,0:T(8,128)(2,1)} %bitcast.229, f32[8,136,128]{2,1,0:T(8,128)} %pad_maximum_fusion.3.out_ref, ...), custom_call_target="tpu_custom_call", output_to_operand_aliasing={{1}: (6, {}), {0}: (7, {})} | custom-call | flops 503316480 | bytes 7077888 | tf_op jit(solution)/shard_map/gb/pallas_call | solution.py:422
  257.6 4.0 convolution_convert_fusion.8
  264.8 6.1 %convolution_convert_fusion.1 = bf16[768,1536]{1,0:T(8,128)(2,1)S(1)} fusion(bf16[2304,768]{1,0:T(8,128)(2,1)S(1)} %copy-done.55, bf16[2304,1536]{1,0:T(8,128)(2,1)S(1)} %bitcast.219), kind=kOutput, calls=%fused_computation.7 | convolution fusion | flops 5436997632 | bytes 12976128 | tf_op jit(solution)/shard_map/dot_general | solution.py:43
  273.9 7.3 %convolution_convert_fusion = bf16[2304,768]{1,0:T(8,128)(2,1)} fusion(bf16[2304,1536]{1,0:T(8,128)(2,1)S(1)} %bitcast.219, bf16[768,1536]{1,0:T(8,128)(2,1)S(1)} %copy-done.1), kind=kOutput, calls=%fused_computation.5 | convolution fusion | flops 5437587456 | bytes 12976128 | tf_op jit(solution)/shard_map/dot_general | solution.py:43
  281.2 6.4 %pb.1 = (bf16[32,64,768]{2,1,0:T(8,128)(2,1)}, bf16[32,64,768]{2,1,0:T(8,128)(2,1)}) custom-call(s32[36]{0:T(128)} %get-tuple-element.190.table_ref, bf16[36,64,768]{2,1,0:T(8,128)(2,1)} %bitcast.223, bf16[12,64,768]{2,1,0:T(8,128)(2,1)} %bitcast.228), custom_call_target="tpu_custom_call" | custom-call | bytes 13369344 | tf_op jit(solution)/shard_map/pb/pallas_call | solution.py:491
  290.3 6.5 %shard_map.355 = (bf16[2,384,768]{2,1,0:T(8,128)(2,1)}, bf16[2,384,768]{2,1,0:T(8,128)(2,1)}, bf16[768,768]{1,0:T(8,128)(2,1)}, bf16[384,768]{1,0:T(8,128)(2,1)}, bf16[384,768]{1,0:T(8,128)(2,1)}) custom-call(s32[1]{0:T(128)} %bitcast.5.where_ref.slot_ref, bf16[768,1536]{1,0:T(8,128)(2,1)} %convolution_convert_fusion.5.refs_0_, ...), custom_call_target="tpu_custom_call" | custom-call | bytes 14155776 | tf_op jit(solution)/shard_map/pallas_call | solution.py:845
  297.7 4.7 shard_map.353
  307.4 3.0 collective-permute-done.79
  314.9 3.8 collective-permute-done.80
  320.4 17.8 %collective-permute-done.83 = f32[2304]{0:T(1024)S(1)} collective-permute-done((f32[2304]{0:T(1024)S(1)}, f32[2304]{0:T(1024)S(1)}, u32[]{:S(2)}, u32[]{:S(2)}) %collective-permute-start.83) | collective-permute-done | bytes 9248 | tf_op jit(solution)/shard_map/ppermute | solution.py:508
  348.4 25.9 %collective-permute-done.46 = bf16[384,384]{1,0:T(8,128)(2,1)} collective-permute-done((bf16[384,384]{1,0:T(8,128)(2,1)}, bf16[384,384]{1,0:T(8,128)(2,1)}, u32[]{:S(2)}, u32[]{:S(2)}) %collective-permute-start.46) | collective-permute-done | bytes 294944 | tf_op jit(solution)/shard_map/ppermute | solution.py:508
  383.3 6.1 %collective-permute-start.50 = (bf16[192,384]{1,0:T(8,128)(2,1)S(1)}, bf16[192,384]{1,0:T(8,128)(2,1)S(1)}, u32[]{:S(2)}, u32[]{:S(2)}) collective-permute-start(bf16[192,384]{1,0:T(8,128)(2,1)S(1)} %get-tuple-element.205), channel_id=1, source_target_pairs={{0,2},{1,3},{2,0},{3,1},{4,6},{5,7},{6,4},{7,5},{8,10},{9,11},{10,... | collective-permute-start | bytes 442376 | tf_op jit(solution)/shard_map/ppermute | solution.py:529
  390.0 4.1 collective-permute-done.50
  396.4 5.2 %shard_map.352 = (bf16[2,256,768]{2,1,0:T(8,128)(2,1)}, bf16[2,256,768]{2,1,0:T(8,128)(2,1)}, bf16[512,768]{1,0:T(8,128)(2,1)}, bf16[256,768]{1,0:T(8,128)(2,1)}, bf16[256,768]{1,0:T(8,128)(2,1)}) custom-call(s32[1]{0:T(128)} %bitcast.5.where_ref.slot_ref, bf16[4,512,768]{2,1,0:T(8,128)(2,1)} %bitcast.225, bf16[4,512,768]{2,1,0:T(8,128)(2,1)} %bitcast.25.refs_1_), custom_call_target="tpu_custom_call" | custom-call | bytes 9437184 | tf_op jit(solution)/shard_map/pallas_call | solution.py:845
  411.6 3.8 collective-permute-start.69
  416.1 7.3 %shard_map.354 = (f32[4,192,768]{2,1,0:T(8,128)}, f32[4,192,768]{2,1,0:T(8,128)}, f32[4,192,768]{2,1,0:T(8,128)}, f32[4,192,768]{2,1,0:T(8,128)}, f32[8,8,768]{2,1,0:T(8,128)}) custom-call(s32[1]{0:T(128)} %bitcast.5.where_ref.slot_ref, bf16[192,384]{1,0:T(8,128)(2,1)} %copy-done.30, bf16[192,384]{1,0:T(8,128)(2,1)} %collective-permute-done.52.refs_1_, ...), custom_call_target="tpu_custom_call" | custom-call | flops 11796480 | bytes 17694720 | tf_op jit(solution)/shard_map/pallas_call | solution.py:927
  425.1 3.0 collective-permute-done.87
  429.4 3.1 collective-permute-done.86
  433.1 5.1 collective-permute-done.85
  438.3 10.7 %collective-permute-done.68 = bf16[192,768]{1,0:T(8,128)(2,1)S(1)} collective-permute-done((bf16[192,768]{1,0:T(8,128)(2,1)S(1)}, bf16[192,768]{1,0:T(8,128)(2,1)S(1)}, u32[]{:S(2)}, u32[]{:S(2)}) %collective-permute-start.68) | collective-permute-done | bytes 294944 | tf_op jit(solution)/shard_map/ppermute | solution.py:529
  456.9 4.0 fusion.89
  463.5 7.5 %collective-permute-done.73.refs_4_ = bf16[96,768]{1,0:T(8,128)(2,1)S(1)} collective-permute-done((bf16[96,768]{1,0:T(8,128)(2,1)S(1)}, bf16[96,768]{1,0:T(8,128)(2,1)S(1)}, u32[]{:S(2)}, u32[]{:S(2)}) %collective-permute-start.73) | collective-permute-done | bytes 147488 | tf_op jit(solution)/shard_map/ppermute | solution.py:508
  477.0 12.6 %shard_map.356 = (f32[2,192,3072]{2,1,0:T(8,128)}, f32[2,192,3072]{2,1,0:T(8,128)}, f32[2,192,3072]{2,1,0:T(8,128)}, f32[2,192,3072]{2,1,0:T(8,128)}, f32[4,8,3072]{2,1,0:T(8,128)}) custom-call(s32[1]{0:T(128)} %bitcast.5.where_ref.slot_ref, bf16[192,768]{1,0:T(8,128)(2,1)} %copy-done.14, bf16[192,768]{1,0:T(8,128)(2,1)} %copy-done.22, ...), custom_call_target="tpu_custom_call" | custom-call | flops 23592960 | bytes 35389440 | tf_op jit(solution)/shard_map/pallas_call | solution.py:927
  494.6 3.2 collective-permute-done.89
  500.1 8.3 %fusion.88 = (bf16[2,192,3072]{2,1,0:T(8,128)(2,1)}, f32[2,192,3072]{2,1,0:T(8,128)}) fusion(f32[2,192,3072]{2,1,0:T(8,128)} %refs_10_.3, f32[2,192,3072]{2,1,0:T(8,128)} %get-tuple-element.139, f32[2]{0:T(128)S(1)} %get-tuple-element.177), kind=kLoop, calls=%fused_computation.284 | loop fusion | flops 3538944 | bytes 16515080 | tf_op jit(solution)/shard_map/convert_element_type | solution.py:917
  (463 shorter events, 167.9 us)
Async XLA Ops:
  0.7 20.8 %collective-permute-start.4 = (bf16[512,768]{1,0:T(8,128)(2,1)}, bf16[512,768]{1,0:T(8,128)(2,1)S(1)}, u32[]{:S(2)}, u32[]{:S(2)}) collective-permute-start(bf16[512,768]{1,0:T(8,128)(2,1)} %bitcast.230), channel_id=1, source_target_pairs={{0,16},{4,20},{8,24},{12,28},{16,0},{20,4},{24,8},{28,12},{1,17},{... | collective-permute-start | bytes 2359304 | tf_op jit(solution)/shard_map/ppermute | solution.py:508
  3.7 22.4 %collective-permute-start.3 = (bf16[512,768]{1,0:T(8,128)(2,1)}, bf16[512,768]{1,0:T(8,128)(2,1)S(1)}, u32[]{:S(2)}, u32[]{:S(2)}) collective-permute-start(bf16[512,768]{1,0:T(8,128)(2,1)} %bitcast.231), channel_id=1, source_target_pairs={{0,8},{4,12},{8,0},{12,4},{16,24},{20,28},{24,16},{28,20},{1,9},{5... | collective-permute-start | bytes 2359304 | tf_op jit(solution)/shard_map/ppermute | solution.py:508
  8.5 18.4 %collective-permute-start.7 = (bf16[208,384]{1,0:T(8,128)(2,1)}, bf16[208,384]{1,0:T(8,128)(2,1)S(1)}, u32[]{:S(2)}, u32[]{:S(2)}) collective-permute-start(bf16[208,384]{1,0:T(8,128)(2,1)} %get-tuple-element.86.refs_0_), channel_id=1, source_target_pairs={{0,3},{1,0},{2,1},{3,2},{4,7},{5,4},{6,5},{7,6},{8,11},{9,8},{10,9... | collective-permute-start | bytes 479240 | tf_op jit(solution)/shard_map/ppermute | solution.py:529
  12.1 15.8 %collective-permute-start.6 = (bf16[208,384]{1,0:T(8,128)(2,1)}, bf16[208,384]{1,0:T(8,128)(2,1)S(1)}, u32[]{:S(2)}, u32[]{:S(2)}) collective-permute-start(bf16[208,384]{1,0:T(8,128)(2,1)} %get-tuple-element.86.refs_0_), channel_id=1, source_target_pairs={{0,2},{1,3},{2,0},{3,1},{4,6},{5,7},{6,4},{7,5},{8,10},{9,11},{10,... | collective-permute-start | bytes 479240 | tf_op jit(solution)/shard_map/ppermute | solution.py:529
  12.1 15.8 %collective-permute-start.5 = (bf16[208,384]{1,0:T(8,128)(2,1)}, bf16[208,384]{1,0:T(8,128)(2,1)S(1)}, u32[]{:S(2)}, u32[]{:S(2)}) collective-permute-start(bf16[208,384]{1,0:T(8,128)(2,1)} %get-tuple-element.86.refs_0_), channel_id=1, source_target_pairs={{0,1},{1,2},{2,3},{3,0},{4,5},{5,6},{6,7},{7,4},{8,9},{9,10},{10,1... | collective-permute-start | bytes 479240 | tf_op jit(solution)/shard_map/ppermute | solution.py:529
  21.5 25.9 %collective-permute-start.2 = (bf16[192,768]{1,0:T(8,128)(2,1)}, bf16[192,768]{1,0:T(8,128)(2,1)}, u32[]{:S(2)}, u32[]{:S(2)}) collective-permute-start(bf16[192,768]{1,0:T(8,128)(2,1)} %get-tuple-element.101.refs_0_), channel_id=1, source_target_pairs={{0,3},{1,0},{2,1},{3,2},{4,7},{5,4},{6,5},{7,6},{8,11},{9,8},{10,9... | collective-permute-start | bytes 884744 | tf_op jit(solution)/shard_map/ppermute | solution.py:529
  26.1 24.6 %collective-permute-start.1 = (bf16[192,768]{1,0:T(8,128)(2,1)}, bf16[192,768]{1,0:T(8,128)(2,1)}, u32[]{:S(2)}, u32[]{:S(2)}) collective-permute-start(bf16[192,768]{1,0:T(8,128)(2,1)} %get-tuple-element.101.refs_0_), channel_id=1, source_target_pairs={{0,2},{1,3},{2,0},{3,1},{4,6},{5,7},{6,4},{7,5},{8,10},{9,11},{10,... | collective-permute-start | bytes 884744 | tf_op jit(solution)/shard_map/ppermute | solution.py:529
  26.9 24.5 %collective-permute-start = (bf16[192,768]{1,0:T(8,128)(2,1)}, bf16[192,768]{1,0:T(8,128)(2,1)}, u32[]{:S(2)}, u32[]{:S(2)}) collective-permute-start(bf16[192,768]{1,0:T(8,128)(2,1)} %get-tuple-element.101.refs_0_), channel_id=1, source_target_pairs={{0,1},{1,2},{2,3},{3,0},{4,5},{5,6},{6,7},{7,4},{8,9},{9,10},{10,1... | collective-permute-start | bytes 884744 | tf_op jit(solution)/shard_map/ppermute | solution.py:529
  30.6 13.6 %collective-permute-start.9 = (bf16[768,384]{1,0:T(8,128)(2,1)}, bf16[768,384]{1,0:T(8,128)(2,1)S(1)}, u32[]{:S(2)}, u32[]{:S(2)}) collective-permute-start(bf16[768,384]{1,0:T(8,128)(2,1)} %get-tuple-element.90.refs_0_), channel_id=1, source_target_pairs={{0,16},{4,20},{8,24},{12,28},{16,0},{20,4},{24,8},{28,12},{1,17},{... | collective-permute-start | bytes 1769480 | tf_op jit(solution)/shard_map/ppermute | solution.py:508
  32.1 13.6 %collective-permute-start.8 = (bf16[768,384]{1,0:T(8,128)(2,1)}, bf16[768,384]{1,0:T(8,128)(2,1)S(1)}, u32[]{:S(2)}, u32[]{:S(2)}) collective-permute-start(bf16[768,384]{1,0:T(8,128)(2,1)} %get-tuple-element.90.refs_0_), channel_id=1, source_target_pairs={{0,8},{4,12},{8,0},{12,4},{16,24},{20,28},{24,16},{28,20},{1,9},{5... | collective-permute-start | bytes 1769480 | tf_op jit(solution)/shard_map/ppermute | solution.py:508
  47.4 19.0 %collective-permute-start.12 = (bf16[768,384]{1,0:T(8,128)(2,1)}, bf16[768,384]{1,0:T(8,128)(2,1)}, u32[]{:S(2)}, u32[]{:S(2)}) collective-permute-start(bf16[768,384]{1,0:T(8,128)(2,1)} %get-tuple-element.90.refs_0_), channel_id=1, source_target_pairs={{0,4},{4,0},{8,12},{12,8},{16,20},{20,16},{24,28},{28,24},{1,5},{5... | collective-permute-start | bytes 1769480 | tf_op jit(solution)/shard_map/ppermute | solution.py:508
  53.5 14.2 %collective-permute-start.14 = (bf16[768,384]{1,0:T(8,128)(2,1)S(1)}, bf16[768,384]{1,0:T(8,128)(2,1)}, u32[]{:S(2)}, u32[]{:S(2)}) collective-permute-start(bf16[768,384]{1,0:T(8,128)(2,1)S(1)} %collective-permute-done.9.refs_2_), channel_id=1, source_target_pairs={{0,4},{4,0},{8,12},{12,8},{16,20},{20,16},{24,28},{28,24},{1,5},{5... | collective-permute-start | bytes 1769480 | tf_op jit(solution)/shard_map/ppermute | solution.py:508
  57.1 10.9 %collective-permute-start.13 = (bf16[768,384]{1,0:T(8,128)(2,1)S(1)}, bf16[768,384]{1,0:T(8,128)(2,1)}, u32[]{:S(2)}, u32[]{:S(2)}) collective-permute-start(bf16[768,384]{1,0:T(8,128)(2,1)S(1)} %collective-permute-done.8.refs_1_), channel_id=1, source_target_pairs={{0,4},{4,0},{8,12},{12,8},{16,20},{20,16},{24,28},{28,24},{1,5},{5... | collective-permute-start | bytes 1769480 | tf_op jit(solution)/shard_map/ppermute | solution.py:508
  66.3 17.4 %collective-permute-start.19 = (bf16[512,768]{1,0:T(8,128)(2,1)S(1)}, bf16[512,768]{1,0:T(8,128)(2,1)}, u32[]{:S(2)}, u32[]{:S(2)}) collective-permute-start(bf16[512,768]{1,0:T(8,128)(2,1)S(1)} %bitcast.234), channel_id=1, source_target_pairs={{0,4},{4,0},{8,12},{12,8},{16,20},{20,16},{24,28},{28,24},{1,5},{5... | collective-permute-start | bytes 2359304 | tf_op jit(solution)/shard_map/ppermute | solution.py:508
  66.4 17.4 %collective-permute-start.21 = (bf16[512,768]{1,0:T(8,128)(2,1)S(1)}, bf16[512,768]{1,0:T(8,128)(2,1)}, u32[]{:S(2)}, u32[]{:S(2)}) collective-permute-start(bf16[512,768]{1,0:T(8,128)(2,1)S(1)} %collective-permute-done.4.refs_2_), channel_id=1, source_target_pairs={{0,4},{4,0},{8,12},{12,8},{16,20},{20,16},{24,28},{28,24},{1,5},{5... | collective-permute-start | bytes 2359304 | tf_op jit(solution)/shard_map/ppermute | solution.py:508
  66.9 17.0 %collective-permute-start.20 = (bf16[512,768]{1,0:T(8,128)(2,1)S(1)}, bf16[512,768]{1,0:T(8,128)(2,1)}, u32[]{:S(2)}, u32[]{:S(2)}) collective-permute-start(bf16[512,768]{1,0:T(8,128)(2,1)S(1)} %collective-permute-done.3.refs_1_), channel_id=1, source_target_pairs={{0,4},{4,0},{8,12},{12,8},{16,20},{20,16},{24,28},{28,24},{1,5},{5... | collective-permute-start | bytes 2359304 | tf_op jit(solution)/shard_map/ppermute | solution.py:508
  67.6 16.2 %collective-permute-start.22 = (bf16[256,768]{1,0:T(8,128)(2,1)}, bf16[256,768]{1,0:T(8,128)(2,1)}, u32[]{:S(2)}, u32[]{:S(2)}) collective-permute-start(bf16[256,768]{1,0:T(8,128)(2,1)} %copy-done.31), channel_id=1, source_target_pairs={{0,4},{4,0},{8,12},{12,8},{16,20},{20,16},{24,28},{28,24},{1,5},{5... | collective-permute-start | bytes 1179656 | tf_op jit(solution)/shard_map/ppermute | solution.py:508
  68.1 15.8 %collective-permute-start.23 = (bf16[256,768]{1,0:T(8,128)(2,1)}, bf16[256,768]{1,0:T(8,128)(2,1)}, u32[]{:S(2)}, u32[]{:S(2)}) collective-permute-start(bf16[256,768]{1,0:T(8,128)(2,1)} %copy-done.32), channel_id=1, source_target_pairs={{0,4},{4,0},{8,12},{12,8},{16,20},{20,16},{24,28},{28,24},{1,5},{5... | collective-permute-start | bytes 1179656 | tf_op jit(solution)/shard_map/ppermute | solution.py:508
  123.4 49.3 %collective-permute-start.31 = (bf16[768,768]{1,0:T(8,128)(2,1)}, bf16[768,768]{1,0:T(8,128)(2,1)}, u32[]{:S(2)}, u32[]{:S(2)}) collective-permute-start(bf16[768,768]{1,0:T(8,128)(2,1)} %get-tuple-element.105.refs_0_), channel_id=1, source_target_pairs={{0,4},{4,0},{8,12},{12,8},{16,20},{20,16},{24,28},{28,24},{1,5},{5... | collective-permute-start | bytes 3538952 | tf_op jit(solution)/shard_map/ppermute | solution.py:508
  123.4 28.7 %collective-permute-start.28 = (bf16[768,768]{1,0:T(8,128)(2,1)}, bf16[768,768]{1,0:T(8,128)(2,1)}, u32[]{:S(2)}, u32[]{:S(2)}) collective-permute-start(bf16[768,768]{1,0:T(8,128)(2,1)} %get-tuple-element.105.refs_0_), channel_id=1, source_target_pairs={{0,16},{4,20},{8,24},{12,28},{16,0},{20,4},{24,8},{28,12},{1,17},{... | collective-permute-start | bytes 3538952 | tf_op jit(solution)/shard_map/ppermute | solution.py:508
  124.7 29.9 %collective-permute-start.27 = (bf16[768,768]{1,0:T(8,128)(2,1)}, bf16[768,768]{1,0:T(8,128)(2,1)}, u32[]{:S(2)}, u32[]{:S(2)}) collective-permute-start(bf16[768,768]{1,0:T(8,128)(2,1)} %get-tuple-element.105.refs_0_), channel_id=1, source_target_pairs={{0,8},{4,12},{8,0},{12,4},{16,24},{20,28},{24,16},{28,20},{1,9},{5... | collective-permute-start | bytes 3538952 | tf_op jit(solution)/shard_map/ppermute | solution.py:508
  126.5 16.6 %collective-permute-start.26 = (f32[4,136,128]{2,1,0:T(8,128)S(1)}, f32[4,136,128]{2,1,0:T(8,128)S(1)}, u32[]{:S(2)}, u32[]{:S(2)}) collective-permute-start(f32[4,136,128]{2,1,0:T(8,128)S(1)} %pad_maximum_fusion.5), channel_id=1, source_target_pairs={{0,4},{4,0},{8,12},{12,8},{16,20},{20,16},{24,28},{28,24},{1,5},{5... | collective-permute-start | bytes 835592 | tf_op jit(solution)/shard_map/ppermute | solution.py:508
  153.2 14.9 %collective-permute-start.30 = (bf16[384,768]{1,0:T(8,128)(2,1)S(1)}, bf16[384,768]{1,0:T(8,128)(2,1)S(1)}, u32[]{:S(2)}, u32[]{:S(2)}) collective-permute-start(bf16[384,768]{1,0:T(8,128)(2,1)S(1)} %slice.313), channel_id=1, source_target_pairs={{0,8},{4,12},{8,0},{12,4},{16,24},{20,28},{24,16},{28,20},{1,9},{5... | collective-permute-start | bytes 1769480 | tf_op jit(solution)/shard_map/ppermute | solution.py:508
  155.6 14.9 %collective-permute-start.29 = (bf16[384,768]{1,0:T(8,128)(2,1)S(1)}, bf16[384,768]{1,0:T(8,128)(2,1)S(1)}, u32[]{:S(2)}, u32[]{:S(2)}) collective-permute-start(bf16[384,768]{1,0:T(8,128)(2,1)S(1)} %slice.312), channel_id=1, source_target_pairs={{0,16},{4,20},{8,24},{12,28},{16,0},{20,4},{24,8},{28,12},{1,17},{... | collective-permute-start | bytes 1769480 | tf_op jit(solution)/shard_map/ppermute | solution.py:508
  157.4 15.3 %collective-permute-start.33 = (bf16[768,768]{1,0:T(8,128)(2,1)}, bf16[768,768]{1,0:T(8,128)(2,1)S(1)}, u32[]{:S(2)}, u32[]{:S(2)}) collective-permute-start(bf16[768,768]{1,0:T(8,128)(2,1)} %collective-permute-done.28.refs_2_), channel_id=1, source_target_pairs={{0,4},{4,0},{8,12},{12,8},{16,20},{20,16},{24,28},{28,24},{1,5},{5... | collective-permute-start | bytes 3538952 | tf_op jit(solution)/shard_map/ppermute | solution.py:508
  157.5 16.3 %collective-permute-start.32 = (bf16[768,768]{1,0:T(8,128)(2,1)}, bf16[768,768]{1,0:T(8,128)(2,1)}, u32[]{:S(2)}, u32[]{:S(2)}) collective-permute-start(bf16[768,768]{1,0:T(8,128)(2,1)} %collective-permute-done.27.refs_1_), channel_id=1, source_target_pairs={{0,4},{4,0},{8,12},{12,8},{16,20},{20,16},{24,28},{28,24},{1,5},{5... | collective-permute-start | bytes 3538952 | tf_op jit(solution)/shard_map/ppermute | solution.py:508
  221.3 27.1 %collective-permute-start.38 = (bf16[2,64,768]{2,1,0:T(8,128)(2,1)S(1)}, bf16[2,64,768]{2,1,0:T(8,128)(2,1)S(1)}, u32[]{:S(2)}, u32[]{:S(2)}) collective-permute-start(bf16[2,64,768]{2,1,0:T(8,128)(2,1)S(1)} %add.546), channel_id=1, source_target_pairs={{0,16},{4,20},{8,24},{12,28},{16,0},{20,4},{24,8},{28,12},{1,17},{... | collective-permute-start | bytes 589832 | tf_op jit(solution)/shard_map/ppermute | solution.py:508
  224.8 65.5 %collective-permute-start.62 = (bf16[768,1536]{1,0:T(8,128)(2,1)}, bf16[768,1536]{1,0:T(8,128)(2,1)}, u32[]{:S(2)}, u32[]{:S(2)}) collective-permute-start(bf16[768,1536]{1,0:T(8,128)(2,1)} %convolution_convert_fusion.2), channel_id=1, source_target_pairs={{0,4},{4,0},{8,12},{12,8},{16,20},{20,16},{24,28},{28,24},{1,5},{5... | collective-permute-start | bytes 7077896 | tf_op jit(solution)/shard_map/ppermute | solution.py:508
  224.8 65.5 %collective-permute-start.61 = (bf16[768,1536]{1,0:T(8,128)(2,1)}, bf16[768,1536]{1,0:T(8,128)(2,1)}, u32[]{:S(2)}, u32[]{:S(2)}) collective-permute-start(bf16[768,1536]{1,0:T(8,128)(2,1)} %convolution_convert_fusion.3), channel_id=1, source_target_pairs={{0,4},{4,0},{8,12},{12,8},{16,20},{20,16},{24,28},{28,24},{1,5},{5... | collective-permute-start | bytes 7077896 | tf_op jit(solution)/shard_map/ppermute | solution.py:508
  273.5 24.2 %collective-permute-start.44 = (bf16[2,768,768]{2,1,0:T(8,128)(2,1)}, bf16[2,768,768]{2,1,0:T(8,128)(2,1)}, u32[]{:S(2)}, u32[]{:S(2)}) collective-permute-start(bf16[2,768,768]{2,1,0:T(8,128)(2,1)} %get-tuple-element.191), channel_id=1, source_target_pairs={{0,4},{4,0},{8,12},{12,8},{16,20},{20,16},{24,28},{28,24},{1,5},{5... | collective-permute-start | bytes 7077896 | tf_op jit(solution)/shard_map/ppermute | solution.py:508
  287.6 108.8 %collective-permute-start.39 = (bf16[32,64,768]{2,1,0:T(8,128)(2,1)}, bf16[32,64,768]{2,1,0:T(8,128)(2,1)}, u32[]{:S(2)}, u32[]{:S(2)}) collective-permute-start(bf16[32,64,768]{2,1,0:T(8,128)(2,1)} %get-tuple-element.117), channel_id=1, source_target_pairs={{0,4},{4,0},{8,12},{12,8},{16,20},{20,16},{24,28},{28,24},{1,5},{5... | collective-permute-start | bytes 9437192 | tf_op jit(solution)/shard_map/ppermute | solution.py:508
  296.9 48.1 %collective-permute-start.63 = (bf16[2,384,768]{2,1,0:T(8,128)(2,1)}, bf16[2,384,768]{2,1,0:T(8,128)(2,1)}, u32[]{:S(2)}, u32[]{:S(2)}) collective-permute-start(bf16[2,384,768]{2,1,0:T(8,128)(2,1)} %get-tuple-element.131), channel_id=1, source_target_pairs={{0,8},{4,12},{8,0},{12,4},{16,24},{20,28},{24,16},{28,20},{1,9},{5... | collective-permute-start | bytes 3538952 | tf_op jit(solution)/shard_map/ppermute | solution.py:508
  302.4 36.4 %collective-permute-start.45 = (bf16[2,384,384]{2,1,0:T(8,128)(2,1)}, bf16[2,384,384]{2,1,0:T(8,128)(2,1)S(1)}, u32[]{:S(2)}, u32[]{:S(2)}) collective-permute-start(bf16[2,384,384]{2,1,0:T(8,128)(2,1)} %get-tuple-element.124), channel_id=1, source_target_pairs={{0,8},{4,12},{8,0},{12,4},{16,24},{20,28},{24,16},{28,20},{1,9},{5... | collective-permute-start | bytes 1769480 | tf_op jit(solution)/shard_map/ppermute | solution.py:508
  304.2 37.8 %collective-permute-start.47 = (bf16[2,384,384]{2,1,0:T(8,128)(2,1)}, bf16[2,384,384]{2,1,0:T(8,128)(2,1)S(1)}, u32[]{:S(2)}, u32[]{:S(2)}) collective-permute-start(bf16[2,384,384]{2,1,0:T(8,128)(2,1)} %get-tuple-element.126), channel_id=1, source_target_pairs={{0,16},{4,20},{8,24},{12,28},{16,0},{20,4},{24,8},{28,12},{1,17},{... | collective-permute-start | bytes 1769480 | tf_op jit(solution)/shard_map/ppermute | solution.py:508
  319.9 18.3 %collective-permute-start.83 = (f32[2304]{0:T(1024)S(1)}, f32[2304]{0:T(1024)S(1)}, u32[]{:S(2)}, u32[]{:S(2)}) collective-permute-start(f32[2304]{0:T(1024)S(1)} %add.587), channel_id=1, source_target_pairs={{0,8},{4,12},{8,0},{12,4},{16,24},{20,28},{24,16},{28,20},{1,9},{5... | collective-permute-start | bytes 27656 | tf_op jit(solution)/shard_map/ppermute | solution.py:508
  338.8 39.5 %collective-permute-start.65 = (bf16[2,384,768]{2,1,0:T(8,128)(2,1)}, bf16[2,384,768]{2,1,0:T(8,128)(2,1)S(1)}, u32[]{:S(2)}, u32[]{:S(2)}) collective-permute-start(bf16[2,384,768]{2,1,0:T(8,128)(2,1)} %get-tuple-element.133), channel_id=1, source_target_pairs={{0,16},{4,20},{8,24},{12,28},{16,0},{20,4},{24,8},{28,12},{1,17},{... | collective-permute-start | bytes 3538952 | tf_op jit(solution)/shard_map/ppermute | solution.py:508
  342.0 32.2 %collective-permute-start.46 = (bf16[384,384]{1,0:T(8,128)(2,1)}, bf16[384,384]{1,0:T(8,128)(2,1)}, u32[]{:S(2)}, u32[]{:S(2)}) collective-permute-start(bf16[384,384]{1,0:T(8,128)(2,1)} %fusion.41), channel_id=1, source_target_pairs={{0,16},{4,20},{8,24},{12,28},{16,0},{20,4},{24,8},{28,12},{1,17},{... | collective-permute-start | bytes 884744 | tf_op jit(solution)/shard_map/ppermute | solution.py:508
  344.6 29.7 %collective-permute-start.48 = (bf16[384,384]{1,0:T(8,128)(2,1)}, bf16[384,384]{1,0:T(8,128)(2,1)}, u32[]{:S(2)}, u32[]{:S(2)}) collective-permute-start(bf16[384,384]{1,0:T(8,128)(2,1)} %fusion.38), channel_id=1, source_target_pairs={{0,8},{4,12},{8,0},{12,4},{16,24},{20,28},{24,16},{28,20},{1,9},{5... | collective-permute-start | bytes 884744 | tf_op jit(solution)/shard_map/ppermute | solution.py:508
  347.2 58.8 %collective-permute-start.64 = (bf16[384,768]{1,0:T(8,128)(2,1)}, bf16[384,768]{1,0:T(8,128)(2,1)S(1)}, u32[]{:S(2)}, u32[]{:S(2)}) collective-permute-start(bf16[384,768]{1,0:T(8,128)(2,1)} %fusion.23), channel_id=1, source_target_pairs={{0,16},{4,20},{8,24},{12,28},{16,0},{20,4},{24,8},{28,12},{1,17},{... | collective-permute-start | bytes 1769480 | tf_op jit(solution)/shard_map/ppermute | solution.py:508
  379.2 26.7 %collective-permute-start.66 = (bf16[384,768]{1,0:T(8,128)(2,1)}, bf16[384,768]{1,0:T(8,128)(2,1)}, u32[]{:S(2)}, u32[]{:S(2)}) collective-permute-start(bf16[384,768]{1,0:T(8,128)(2,1)} %fusion.20), channel_id=1, source_target_pairs={{0,8},{4,12},{8,0},{12,4},{16,24},{20,28},{24,16},{28,20},{1,9},{5... | collective-permute-start | bytes 1769480 | tf_op jit(solution)/shard_map/ppermute | solution.py:508
  408.6 44.1 %collective-permute-start.40 = (bf16[2,256,768]{2,1,0:T(8,128)(2,1)}, bf16[2,256,768]{2,1,0:T(8,128)(2,1)}, u32[]{:S(2)}, u32[]{:S(2)}) collective-permute-start(bf16[2,256,768]{2,1,0:T(8,128)(2,1)} %get-tuple-element.119), channel_id=1, source_target_pairs={{0,8},{4,12},{8,0},{12,4},{16,24},{20,28},{24,16},{28,20},{1,9},{5... | collective-permute-start | bytes 2359304 | tf_op jit(solution)/shard_map/ppermute | solution.py:508
  410.6 44.9 %collective-permute-start.42 = (bf16[2,256,768]{2,1,0:T(8,128)(2,1)}, bf16[2,256,768]{2,1,0:T(8,128)(2,1)}, u32[]{:S(2)}, u32[]{:S(2)}) collective-permute-start(bf16[2,256,768]{2,1,0:T(8,128)(2,1)} %get-tuple-element.121), channel_id=1, source_target_pairs={{0,16},{4,20},{8,24},{12,28},{16,0},{20,4},{24,8},{28,12},{1,17},{... | collective-permute-start | bytes 2359304 | tf_op jit(solution)/shard_map/ppermute | solution.py:508
  411.6 26.6 %collective-permute-start.67 = (bf16[192,768]{1,0:T(8,128)(2,1)}, bf16[192,768]{1,0:T(8,128)(2,1)}, u32[]{:S(2)}, u32[]{:S(2)}) collective-permute-start(bf16[192,768]{1,0:T(8,128)(2,1)} %get-tuple-element.196), channel_id=1, source_target_pairs={{0,1},{1,2},{2,3},{3,0},{4,5},{5,6},{6,7},{7,4},{8,9},{9,10},{10,1... | collective-permute-start | bytes 884744 | tf_op jit(solution)/shard_map/ppermute | solution.py:529
  411.6 26.6 %collective-permute-start.69 = (bf16[192,768]{1,0:T(8,128)(2,1)S(1)}, bf16[192,768]{1,0:T(8,128)(2,1)}, u32[]{:S(2)}, u32[]{:S(2)}) collective-permute-start(bf16[192,768]{1,0:T(8,128)(2,1)S(1)} %get-tuple-element.197), channel_id=1, source_target_pairs={{0,3},{1,0},{2,1},{3,2},{4,7},{5,4},{6,5},{7,6},{8,11},{9,8},{10,9... | collective-permute-start | bytes 884744 | tf_op jit(solution)/shard_map/ppermute | solution.py:529
  451.8 11.1 %collective-permute-start.70 = (bf16[192,768]{1,0:T(8,128)(2,1)S(1)}, bf16[192,768]{1,0:T(8,128)(2,1)S(1)}, u32[]{:S(2)}, u32[]{:S(2)}) collective-permute-start(bf16[192,768]{1,0:T(8,128)(2,1)S(1)} %fusion.37.refs_0_), channel_id=1, source_target_pairs={{0,8},{4,12},{8,0},{12,4},{16,24},{20,28},{24,16},{28,20},{1,9},{5... | collective-permute-start | bytes 884744 | tf_op jit(solution)/shard_map/ppermute | solution.py:508
  453.9 17.7 %collective-permute-start.41 = (bf16[256,768]{1,0:T(8,128)(2,1)S(1)}, bf16[256,768]{1,0:T(8,128)(2,1)S(1)}, u32[]{:S(2)}, u32[]{:S(2)}) collective-permute-start(bf16[256,768]{1,0:T(8,128)(2,1)S(1)} %fusion.32), channel_id=1, source_target_pairs={{0,16},{4,20},{8,24},{12,28},{16,0},{20,4},{24,8},{28,12},{1,17},{... | collective-permute-start | bytes 1179656 | tf_op jit(solution)/shard_map/ppermute | solution.py:508
  456.7 14.9 %collective-permute-start.43 = (bf16[256,768]{1,0:T(8,128)(2,1)S(1)}, bf16[256,768]{1,0:T(8,128)(2,1)S(1)}, u32[]{:S(2)}, u32[]{:S(2)}) collective-permute-start(bf16[256,768]{1,0:T(8,128)(2,1)S(1)} %fusion.30), channel_id=1, source_target_pairs={{0,8},{4,12},{8,0},{12,4},{16,24},{20,28},{24,16},{28,20},{1,9},{5... | collective-permute-start | bytes 1179656 | tf_op jit(solution)/shard_map/ppermute | solution.py:508
  463.5 11.4 %collective-permute-start.74 = (bf16[192,768]{1,0:T(8,128)(2,1)S(1)}, bf16[192,768]{1,0:T(8,128)(2,1)S(1)}, u32[]{:S(2)}, u32[]{:S(2)}) collective-permute-start(bf16[192,768]{1,0:T(8,128)(2,1)S(1)} %fusion.37.refs_0_), channel_id=1, source_target_pairs={{0,4},{4,0},{8,12},{12,8},{16,20},{20,16},{24,28},{28,24},{1,5},{5... | collective-permute-start | bytes 884744 | tf_op jit(solution)/shard_map/ppermute | solution.py:508
  (121 other events, 1153.7 us)
where the time goes:
time: 514 us; the launch traced here: 509 us
  waiting for transfers between devices  147 us (29%)
  Pallas kernels  141 us (27%)
  starting transfers between devices  83.5 us (16%)
  other arithmetic  54.3 us (11%)
  matrix products  44.8 us (9%)
  local copies, waits for them, and re-layouts  34.3 us (7%)
    ppermute x70, waiting for transfers between devices, exchange(): return lax.ppermute(value, CTX, [(i, i ^ mask) for i in range(count)])  102 us
    ppermute x70, starting transfers between devices, exchange(): return lax.ppermute(value, CTX, [(i, i ^ mask) for i in range(count)])  49.5 us
    dot_general x15, matrix products, mm(): return lax.dot_general(a, b, dims, preferred_element_type=F32)  44.8 us
    ppermute x21, waiting for transfers between devices, wa_shift(): lax.ppermute(value, WA, [(i, (i + step) % count) for i in range(count)])  44.7 us
    ppermute x21, starting transfers between devices, wa_shift(): lax.ppermute(value, WA, [(i, (i + step) % count) for i in range(count)])  34 us
    pallas_call x1, Pallas kernels, sparse_bwd(): pl.pallas_call(sparse_bwd_kernel, grid_spec=pltpu.PrefetchScalarGridSpec(...  23 us
    pallas_call x2, Pallas kernels, adam(): pl.pallas_call(functools.partial(adam_kernel, pieces=piece_columns // CUT...  19.9 us
    pallas_call x3, Pallas kernels, spread(): pl.pallas_call(functools.partial(spread_kernel, read=read), grid_spec=plt...  16.4 us
  transfers between devices with their start and end apart: 91, of which 28 were waited for; matrix products, arithmetic and copies ran while one was open for 18% of the time, Pallas kernels for 17%

commit v1 on v0

--- a/solution.py
+++ b/solution.py
@@ -19,6 +19,7 @@
 PAIR = 2 * HEAD
 QUADS = HEADS // 4
 QUAD = 4 * HEAD
+EACH = 6
 
 MASKED_SCORE = -1e30
 LN_EPS = 1e-06
@@ -104,36 +105,71 @@
         lse_ref[0, h : h + 1, :] = top + jnp.log(total)
 
 
-def sparse_bwd_kernel(
-    nvalid_ref, q_ref, do_ref, lse_ref, near_ref, rand_ref, dq_ref, grads_ref, acc_ref
+def attention_bwd_kernel(
+    nvalid_ref, q_ref, do_ref, lse_ref, near_ref, rand_ref, gq_ref, gdo_ref, gdo_in_ref, gout_ref,
+    dq_ref, grads_ref, acc_ref
 ):
     i = pl.program_id(0)
+    blocks = near_ref.shape[0] - FRINGE
+    rows = gq_ref.shape[0]
+    keys = blocks * BLOCK
 
     @pl.when(i == 0)
     def _():
         acc_ref[...] = jnp.zeros_like(acc_ref)
-
-    blocks = near_ref.shape[0] - FRINGE
-    places = window_places(i, blocks) + (blocks + 2, blocks + 3)
-    for h in range(QUADS):
-        cols = slice(h * QUAD, (h + 1) * QUAD)
-        vcols = slice(D + h * QUAD, D + (h + 1) * QUAD)
-        queries = heads_apart(q_ref[:, cols])
-        douts = heads_apart(do_ref[:, cols])
-        k = slot_rows(near_ref, rand_ref, i, cols)
-        v = slot_rows(near_ref, rand_ref, i, vcols)
-        s = slot_scores(k, queries, nvalid_ref, i * 3)
-        p = jnp.exp(s - lse_ref[0, h : h + 1, :])
-        dp = mm(v, douts, NT)
-        ds = (p * (dp - jnp.sum(p * dp, axis=0, keepdims=True))).astype(BF16)
-        dq = heads_joined(mm(ds, k, TN)) * (HEAD**-0.5)
-        dq_ref[:, cols] = dq.astype(BF16)
-        dk = mm(ds, queries).reshape(SLOTS, BLOCK, QUAD)
-        dv = mm(p.astype(BF16), douts).reshape(SLOTS, BLOCK, QUAD)
-        for grad, to in ((dk, cols), (dv, vcols)):
-            for at, place in enumerate(places):
-                acc_ref[place, :, to] += grad[at]
-            grads_ref[:, :, to] = grad[len(places) :].astype(BF16)
+        dq_ref[keys:] = jnp.zeros((FRINGE * BLOCK, D), BF16)
+
+    @pl.when(i < blocks)
+    def _():
+        places = window_places(i, blocks) + (blocks + 2, blocks + 3)
+        for h in range(QUADS):
+            cols = slice(h * QUAD, (h + 1) * QUAD)
+            vcols = slice(D + h * QUAD, D + (h + 1) * QUAD)
+            queries = heads_apart(q_ref[:, cols])
+            douts = heads_apart(do_ref[:, cols])
+            k = slot_rows(near_ref, rand_ref, i, cols)
+            v = slot_rows(near_ref, rand_ref, i, vcols)
+            s = slot_scores(k, queries, nvalid_ref, i * 3)
+            p = jnp.exp(s - lse_ref[0, h : h + 1, :])
+            dp = mm(v, douts, NT)
+            ds = (p * (dp - jnp.sum(p * dp, axis=0, keepdims=True))).astype(BF16)
+            dq = heads_joined(mm(ds, k, TN)) * (HEAD**-0.5)
+            dq_ref[pl.ds(pl.multiple_of(i * BLOCK, BLOCK), BLOCK), cols] = dq.astype(BF16)
+            dk = mm(ds, queries).reshape(SLOTS, BLOCK, QUAD)
+            dv = mm(p.astype(BF16), douts).reshape(SLOTS, BLOCK, QUAD)
+            for grad, to in ((dk, cols), (dv, vcols)):
+                for at, place in enumerate(places):
+                    acc_ref[place, :, to] += grad[at]
+                grads_ref[:, :, to] = grad[len(places) :].astype(BF16)
+
+    @pl.when(i == blocks)
+    def _():
+        ok = lax.broadcasted_iota(jnp.int32, (keys, 2 * rows), 0) < nvalid_ref[blocks * 3]
+
+        @pl.loop(0, PAIRS)
+        def _(h):
+            cols = pl.ds(pl.multiple_of(h * PAIR, PAIR), PAIR)
+            vcols = pl.ds(pl.multiple_of(D + h * PAIR, PAIR), PAIR)
+            queries = heads_apart(gq_ref[:, cols])
+            douts = heads_apart(gdo_ref[:, cols] + gdo_in_ref[:, cols])
+            out = gout_ref[h, :rows]
+            outs = jnp.concatenate([out, out], axis=0)
+            dot = jnp.sum((douts.astype(F32) * outs).T, axis=0, keepdims=True)
+            lse = jnp.concatenate(
+                [gout_ref[h, rows : rows + 1], gout_ref[h, rows + 1 : rows + 2]], axis=1
+            )
+            k = near_ref[:blocks, :, cols].reshape(keys, PAIR)
+            v = near_ref[:blocks, :, vcols].reshape(keys, PAIR)
+            p = jnp.where(ok, jnp.exp(mm(k, queries, NT) - lse), 0.0)
+            ds = (p * (mm(v, douts, NT) - dot)).astype(BF16)
+            dq = heads_joined(mm(ds, k, TN)) * (HEAD**-0.5)
+            dq_ref[keys + FRINGE * BLOCK - rows :, cols] = dq.astype(BF16)
+            acc_ref[:blocks, :, cols] += mm(ds, queries).reshape(blocks, BLOCK, PAIR)
+            acc_ref[:blocks, :, vcols] += mm(p.astype(BF16), douts).reshape(blocks, BLOCK, PAIR)
+
+    @pl.when(i >= blocks)
+    def _():
+        grads_ref[...] = acc_ref[pl.ds((i - blocks) * RAND, RAND)].astype(BF16)
 
 
 def piece_copies(held, slot, buf_ref, sems, to):
@@ -201,72 +237,29 @@
         out_ref[rows + 2 :] = jnp.zeros((6, PAIR), F32)
 
 
-def global_bwd_kernel(
-    nvalid_ref, q_ref, do_ref, out_ref, kv_ref, near_ref, used_ref, own_ref, dq_ref, res_ref
-):
-    rows = q_ref.shape[0]
-    keys = kv_ref.shape[0]
-    ok = lax.broadcasted_iota(jnp.int32, (keys, 2 * rows), 0) < nvalid_ref[0]
-    dq_ref[:rows] = jnp.zeros((rows, D), BF16)
-    for h in range(PAIRS):
-        cols = slice(h * PAIR, (h + 1) * PAIR)
-        vcols = slice(D + h * PAIR, D + (h + 1) * PAIR)
-        queries = heads_apart(q_ref[:, cols])
-        douts = heads_apart(do_ref[:, cols])
-        outs = jnp.concatenate([out_ref[h, :rows], out_ref[h, :rows]], axis=0)
-        dot = jnp.sum((douts.astype(F32) * outs).T, axis=0, keepdims=True)
-        lse = jnp.concatenate(
-            [out_ref[h, rows : rows + 1], out_ref[h, rows + 1 : rows + 2]], axis=1
-        )
-        k = kv_ref[:, cols]
-        v = kv_ref[:, vcols]
-        p = jnp.where(ok, jnp.exp(mm(k, queries, NT) - lse), 0.0)
-        ds = (p * (mm(v, douts, NT) - dot)).astype(BF16)
-        dq = heads_joined(mm(ds, k, TN)) * (HEAD**-0.5)
-        dq_ref[rows:, cols] = dq.astype(BF16)
-        for grad, at in ((mm(ds, queries), cols), (mm(p.astype(BF16), douts), vcols)):
-            res_ref[:keys, at] = (near_ref[:keys, at] + grad).astype(BF16)
-            res_ref[keys:, at] = near_ref[keys:, at].astype(BF16)
-
-
-def kv_used_kernel(source_ref, index_ref, w_ref, b_ref, *refs):
+def kv_used_kernel(start_ref, order_ref, index_ref, w_ref, b_ref, *refs):
     held = refs[:-4]
     kv_ref, x_ref, buf_ref, sems = refs[-4:]
     step = pl.program_id(0)
-    count = buf_ref.shape[1] // BLOCK
-
-    def rows_of(to, at):
-        return buf_ref.at[to, pl.ds(at * BLOCK, BLOCK)]
-
-    def fetch(group, to):
-        for at in range(count):
-            place = group * count + at
-            for which, ref in enumerate(held):
-
-                @pl.when(source_ref[place] == which)
-                def _():
-                    start = pl.multiple_of(index_ref[place] * BLOCK, BLOCK)
-                    pltpu.make_async_copy(
-                        ref.at[pl.ds(start, BLOCK)], rows_of(to, at), sems.at[to, at]
-                    ).start()
-
-    now = lax.rem(step, 2)
+    each = x_ref.shape[0] // BLOCK
+
+    def copy(ref, start, at):
+        start = pl.multiple_of(start * BLOCK, BLOCK)
+        return pltpu.make_async_copy(ref.at[pl.ds(start, BLOCK)], buf_ref.at[at], sems.at[at])
 
     @pl.when(step == 0)
     def _():
-        fetch(0, 0)
-
-    @pl.when(step + 1 < pl.num_programs(0))
-    def _():
-        fetch(step + 1, 1 - now)
-
-    for at in range(count):
-        pltpu.make_async_copy(
-            held[0].at[pl.ds(0, BLOCK)], rows_of(now, at), sems.at[now, at]
-        ).wait()
-    rows = buf_ref[now]
-    x_ref[...] = rows
-    kv_ref[...] = (mm(rows, w_ref[...]) + b_ref[...]).astype(BF16)
+        for which, ref in enumerate(held):
+
+            @pl.loop(start_ref[which], start_ref[which + 1])
+            def _(n):
+                copy(ref, index_ref[n], order_ref[n]).start()
+
+    for at in range(each):
+        copy(held[0], 0, step * each + at).wait()
+    x_ref[...] = buf_ref[pl.ds(step * each, each)].reshape(each * BLOCK, D)
+
+    kv_ref[...] = (mm(x_ref[...], w_ref[...]) + b_ref[...]).astype(BF16)
 
 
 def place_blocks_kernel(table_ref, x_ref, q_ref, low_ref, high_ref):
@@ -274,9 +267,8 @@
     high_ref[...] = jnp.zeros_like(high_ref)
     limit = low_ref.shape[0]
 
-    def step(s, with_query):
+    def step(s, part):
         to = table_ref[s]
-        part = x_ref[s] + q_ref[s] if with_query else x_ref[s]
 
         @pl.when(to < limit)
         def _():
@@ -288,11 +280,11 @@
 
     @pl.loop(0, q_ref.shape[0])
     def _(s):
-        step(s, True)
+        step(s, x_ref[s] + q_ref[s])
 
     @pl.loop(q_ref.shape[0], x_ref.shape[0])
     def _(s):
-        step(s, False)
+        step(s, x_ref[s])
 
 
 def whole(shape):
@@ -344,38 +336,47 @@
     )(nvalid, q, kv_used, kv_used)
 
 
-def sparse_bwd(nvalid, q, dout, lse, kv_used):
+def attention_bwd(nvalid, q, dout, lse, kv_used, glob_q, glob_do, glob_do_in, glob_out):
     rows = q.shape[0]
     blocks = rows // BLOCK
     near = blocks + FRINGE
-    used = kv_used.shape[0]
-    work = 2 * rows * SLOTS * BLOCK * D
+    last = blocks - 1
+    glob = glob_q.shape[0]
+    work = 2 * (rows + glob) * SLOTS * BLOCK * D
+    each = pl.BlockSpec((BLOCK, D), lambda i, n: (jnp.minimum(i, last), 0))
+    rand = (RAND, BLOCK, 2 * D)
     return pl.pallas_call(
-        sparse_bwd_kernel,
+        attention_bwd_kernel,
         grid_spec=pltpu.PrefetchScalarGridSpec(
             num_scalar_prefetch=1,
-            grid=(blocks,),
+            grid=(blocks + near // RAND,),
             in_specs=[
-                pl.BlockSpec((BLOCK, D), lambda i, n: (i, 0)),
-                pl.BlockSpec((BLOCK, D), lambda i, n: (i, 0)),
-                pl.BlockSpec((1, 8, QUAD), lambda i, n: (i, 0, 0)),
+                each,
+                each,
+                pl.BlockSpec((1, 8, QUAD), lambda i, n: (jnp.minimum(i, last), 0, 0)),
                 near_spec(near),
-                rand_spec(near),
+                pl.BlockSpec(rand, lambda i, n: (near // RAND + jnp.minimum(i, last), 0, 0)),
+                whole((glob, D)),
+                whole((glob, D)),
+                whole((glob, D)),
+                whole(glob_out.shape),
             ],
             out_specs=[
-                pl.BlockSpec((BLOCK, D), lambda i, n: (i, 0)),
-                rand_spec(near),
-                near_spec(near),
+                whole((near * BLOCK, D)),
+                pl.BlockSpec(
+                    rand,
+                    lambda i, n: (jnp.where(i < blocks, near // RAND + i, i - blocks), 0, 0),
+                ),
             ],
+            scratch_shapes=[pltpu.VMEM((near, BLOCK, 2 * D), F32)],
         ),
         out_shape=[
             jax.ShapeDtypeStruct((near * BLOCK, D), BF16),
-            jax.ShapeDtypeStruct((used, BLOCK, 2 * D), BF16),
-            jax.ShapeDtypeStruct((near, BLOCK, 2 * D), F32),
+            jax.ShapeDtypeStruct(kv_used.shape, BF16),
         ],
         cost_estimate=cost(5 * work, rows * SLOTS * D * 8, rows * SLOTS * BLOCK * HEADS),
         name="sb",
-    )(nvalid, q, dout, lse, kv_used, kv_used)
+    )(nvalid, q, dout, lse, kv_used, kv_used, glob_q, glob_do, glob_do_in, glob_out)
 
 
 def global_fwd(pair, nvalid, q, w_kv, kv_bias, held):
@@ -412,59 +413,24 @@
     )(pair[None], nvalid, q, w_kv, w_kv, kv_bias, *held)
 
 
-def global_bwd(nvalid, q, dout, out, kv_used, near, used, dq):
-    rows = q.shape[0]
-    near_rows = near.shape[0] * BLOCK
-    keys = near_rows - FRINGE * BLOCK
-    near = near.reshape(near_rows, 2 * D)
-    used_rows = used.shape[0] * BLOCK
-    fringe = FRINGE * BLOCK
-    return pl.pallas_call(
-        global_bwd_kernel,
-        grid_spec=pltpu.PrefetchScalarGridSpec(
-            num_scalar_prefetch=1,
-            grid=(1,),
-            in_specs=[
-                whole((rows, D)),
-                whole((rows, D)),
-                whole(out.shape),
-                whole((keys, 2 * D)),
-                whole((near_rows, 2 * D)),
-                pl.BlockSpec(memory_space=pl.ANY),
-                pl.BlockSpec(memory_space=pl.ANY),
-            ],
-            out_specs=[
-                pl.BlockSpec((fringe, D), lambda i, n: (keys // fringe, 0)),
-                whole((near_rows, 2 * D)),
-            ],
-        ),
-        out_shape=[
-            jax.ShapeDtypeStruct((near_rows, D), BF16),
-            jax.ShapeDtypeStruct((used_rows, 2 * D), BF16),
-        ],
-        input_output_aliases={6: 1, 7: 0},
-        cost_estimate=cost(10 * rows * keys * D, near_rows * D * 12, rows * keys * HEADS),
-        name="gb",
-    )(
-        nvalid,
-        q,
-        dout,
-        out,
-        kv_used.reshape(used_rows, 2 * D),
-        near,
-        used.reshape(used_rows, 2 * D),
-        dq,
-    )
-
-
 def kv_used_rows(source, index, w_kv, kv_bias, held):
     count = source.shape[0]
-    each = 4
+    each = EACH
     rows = each * BLOCK
+    number = jnp.arange(count, dtype=jnp.int32)
+    earlier = (source[None] < source[:, None]) | (
+        (source[None] == source[:, None]) & (number[None] < number[:, None])
+    )
+    rank = jnp.sum(earlier, axis=1, dtype=jnp.int32)
+    chosen = (rank[None] == number[:, None]).astype(jnp.int32)
+    order = jnp.sum(chosen * number[None], axis=1, dtype=jnp.int32)
+    places = jnp.sum(chosen * index[None], axis=1, dtype=jnp.int32)
+    sources = jnp.arange(len(held) + 1, dtype=jnp.int32)
+    starts = jnp.sum(source[None] < sources[:, None], axis=1, dtype=jnp.int32)
     return pl.pallas_call(
         kv_used_kernel,
         grid_spec=pltpu.PrefetchScalarGridSpec(
-            num_scalar_prefetch=2,
+            num_scalar_prefetch=3,
             grid=(count // each,),
             in_specs=[whole((D, 2 * D)), whole((1, 2 * D))]
             + [pl.BlockSpec(memory_space=pl.ANY)] * len(held),
@@ -473,8 +439,8 @@
                 pl.BlockSpec((rows, D), lambda t, *a: (t, 0)),
             ],
             scratch_shapes=[
-                pltpu.VMEM((2, rows, D), BF16),
-                pltpu.SemaphoreType.DMA((2, each)),
+                pltpu.VMEM((count, BLOCK, D), BF16),
+                pltpu.SemaphoreType.DMA((count,)),
             ],
         ),
         out_shape=[
@@ -483,7 +449,7 @@
         ],
         cost_estimate=cost(4 * count * BLOCK * D * D, 8 * count * BLOCK * D),
         name="kv",
-    )(source, index, w_kv, kv_bias, *held)
+    )(starts, order, places, w_kv, kv_bias, *held)
 
 
 def place_blocks(table, x_blocks, q_blocks, total):
@@ -549,12 +515,12 @@
 
 def wa_total(value):
     count = lax.axis_size(WA)
-    rank = lax.axis_index(WA)
-    parts = jnp.stack(wa_parts(value))
-    total = parts[rank % count]
-    for index in range(1, count):
-        total = total + parts[(rank - index) % count]
-    return total
+    mask = 1
+    while mask < count:
+        pairs = [(i, i ^ mask) for i in range(count)]
+        value = value + lax.ppermute(value, WA, pairs)
+        mask *= 2
+    return value
 
 
 def bit_of(mask):
@@ -573,6 +539,11 @@
     near = [own, first, second, upper, lower]
     held = near + [exchange(part, CORE) for part in near]
     return held if then is None else (held, then)
+
+
+def gather_direct(own):
+    near = [own] + [exchange(own, mask) for mask in (FIRST, SECOND, FIRST | SECOND)]
+    return near + [exchange(part, CORE) for part in near]
 
 
 def group_in_order(own):
@@ -713,11 +684,13 @@
 
 def matrix_copies(held, step, up_ref, down_ref, sems, to):
     jobs = []
+    half = D // 2
     for at in range(STRIDE):
         side, place = divmod(step * STRIDE + at, 4)
         own, first, second, upper, lower = held[5 * side : 5 * side + 5]
-        half = D // 2
-        parts = [((own, first, second)[place], 0, D)] if place < 3 else [(upper, 0, half), (lower, half, half)]
+        parts = [(upper, 0, half), (lower, half, half)]
+        if place < 3:
+            parts = [((own, first, second)[place], 0, D)]
         for ref, start, size in parts:
             for which, buf in enumerate((up_ref, down_ref)):
                 source = ref.at[:, pl.ds(which * CUT, CUT)]
@@ -797,26 +770,9 @@
 
 
 def spread_kernel(slot_ref, *refs, read):
-    keep = refs[: len(refs) - 5]
-    x_ref, y_ref, own_ref, first_ref, second_ref = refs[len(refs) - 5 :]
-    upper = pl.program_id(0) < pl.num_programs(0) // 2
-
-    def part(slot):
-        return read(slot_ref, keep, slot).astype(BF16)
-
-    own_ref[...] = part(0)
-
-    @pl.when(upper)
-    def _():
-        x_ref[0] = part(3)
-        x_ref[1] = part(1)
-        second_ref[...] = part(2)
-
-    @pl.when(jnp.logical_not(upper))
-    def _():
-        y_ref[0] = part(3)
-        y_ref[1] = part(2)
-        first_ref[...] = part(1)
+    keep, outs = refs[:-4], refs[-4:]
+    for slot, out in enumerate(outs):
+        out[...] = read(slot_ref, keep, slot).astype(BF16)
 
 
 def read_ffn(slot_ref, refs, slot):
@@ -836,48 +792,29 @@
 
 
 def spread(slot, arrays, in_specs, rows, columns, read, tiles):
-    size = rows // tiles
-    middle = tiles // 2
-    low = lambda t: jnp.minimum(t, middle - 1)
-    high = lambda t: jnp.maximum(t - middle, 0)
-    half = jax.ShapeDtypeStruct((rows // 2, columns), BF16)
-    pair = jax.ShapeDtypeStruct((2, rows // 2, columns), BF16)
+    block = pl.BlockSpec((rows // tiles, columns), lambda t, *a: (t, 0))
     return pl.pallas_call(
         functools.partial(spread_kernel, read=read),
         grid_spec=pltpu.PrefetchScalarGridSpec(
-            num_scalar_prefetch=1,
-            grid=(tiles,),
-            in_specs=in_specs,
-            out_specs=[
-                pl.BlockSpec((2, size, columns), lambda t, *a: (0, low(t), 0)),
-                pl.BlockSpec((2, size, columns), lambda t, *a: (0, high(t), 0)),
-                pl.BlockSpec((size, columns), lambda t, *a: (t, 0)),
-                pl.BlockSpec((size, columns), lambda t, *a: (high(t), 0)),
-                pl.BlockSpec((size, columns), lambda t, *a: (low(t), 0)),
-            ],
+            num_scalar_prefetch=1, grid=(tiles,), in_specs=in_specs, out_specs=[block] * 4
         ),
-        out_shape=[pair, pair, jax.ShapeDtypeStruct((rows, columns), BF16), half, half],
+        out_shape=[jax.ShapeDtypeStruct((rows, columns), BF16)] * 4,
         cost_estimate=cost(0, rows * columns * 24),
     )(slot[None], *arrays)
 
 
 def reduce_group(slot, arrays, in_specs, rows, columns, read, tiles=4):
-    x_out, y_out, own, first, second = spread(slot, arrays, in_specs, rows, columns, read, tiles)
-    x_in = exchange(x_out, FIRST)
-    y_in = exchange(y_out, SECOND)
-    x_last = exchange(add_low(first, y_in[0]), FIRST)
-    y_last = exchange(add_low(second, x_in[0]), SECOND)
-    cut = rows // 2
-    upper = own[:cut].astype(F32) + x_in[1].astype(F32) + y_last.astype(F32)
-    lower = own[cut:].astype(F32) + y_in[1].astype(F32) + x_last.astype(F32)
-    return upper, lower
+    own, *others = spread(slot, arrays, in_specs, rows, columns, read, tiles)
+    total = own.astype(F32)
+    for part, mask in zip(others, (FIRST, SECOND, FIRST | SECOND)):
+        total = total + exchange(part, mask).astype(F32)
+    return total
 
 
 def adam_kernel(slot_ref, *refs, pieces):
-    held = refs[:10]
-    w_ref, m_ref, v_ref, grad_ref, first_ref, second_ref, step_ref, sums_ref = refs[10:]
-
-    def body(slot, ref):
+    held = refs[:GROUP]
+    w_ref, m_ref, v_ref, grad_ref, first_ref, second_ref, step_ref, sums_ref = refs[GROUP:]
+    for slot, ref in enumerate(held):
         at = slot_ref[0] ^ slot
         if pieces == 1:
             columns = pl.ds(pl.multiple_of(at % 2 * CUT, 128), CUT)
@@ -886,8 +823,6 @@
             columns = pl.ds(pl.multiple_of(at * CUT, 128), CUT)
             grad_ref[0, :, columns] = ref[:, :CUT].astype(F32)
             grad_ref[1, :, columns] = ref[:, CUT:].astype(F32)
-
-    for_each_slot(held, body)
 
     @pl.when(pl.program_id(0) == 0)
     def _():
@@ -907,13 +842,13 @@
         move = first / (jnp.sqrt(second) + ADAM_EPS) + WEIGHT_DECAY * weight
         first_ref[mat, here] = first
         second_ref[mat, here] = second
-        step_ref[mat, here] = move
+        step_ref[mat, here] = move.astype(BF16)
         for row, part in ((mat, weight), (mats + mat, move)):
             sums_ref[row] += jnp.sum((part * part).reshape(each // 8, 8, columns), axis=0)
 
 
 def final(ratios, master, step):
-    new = master - (STEP_RATE * ratios)[:, None, None] * step
+    new = master - (STEP_RATE * ratios)[:, None, None] * step.astype(F32)
     return new, new.astype(BF16)
 
 
@@ -929,10 +864,15 @@
         grid_spec=pltpu.PrefetchScalarGridSpec(
             num_scalar_prefetch=1,
             grid=(tiles,),
-            in_specs=held_specs(wide, piece_columns, tiles) + [block] * 3,
+            in_specs=[pl.BlockSpec((size, piece_columns), lambda t, *a: (t, 0))] * GROUP
+            + [block] * 3,
             out_specs=[block] * 4 + [whole((2 * mats, 8, columns))],
         ),
-        out_shape=[full] * 4 + [jax.ShapeDtypeStruct((2 * mats, 8, columns), F32)],
+        out_shape=[full] * 3
+        + [
+            jax.ShapeDtypeStruct(master.shape, BF16),
+            jax.ShapeDtypeStruct((2 * mats, 8, columns), F32),
+        ],
         cost_estimate=cost(20 * master.size, 30 * master.size, master.size),
     )(slot[None], *held, master, first, second)
 
@@ -1086,14 +1026,17 @@
     tiles = 4
     ffn_spec = pl.BlockSpec((D // tiles, cut), lambda t, *a: (t, 0))
 
-    def finish(upper, lower):
-        total = jnp.concatenate([upper, lower], axis=0).astype(BF16)
+    def finish(total, extra=None):
+        total = total.astype(BF16)
         for mask in spare_masks():
             total = add_low(total, exchange(total, mask))
-        return wa_reduce(total.reshape(wa_count, wide, total.shape[1])).astype(BF16)
+        total = total.reshape(wa_count, wide, total.shape[1])
+        if extra is not None:
+            total = jnp.concatenate([total, extra], axis=1)
+        return wa_reduce(total)
 
     ffn_mine = finish(
-        *reduce_group(
+        reduce_group(
             my_slot,
             [up_keep, down_keep, exchange(up_sent, CORE), exchange(down_sent, CORE)],
             [ffn_spec] * 4,
@@ -1102,23 +1045,31 @@
             read_ffn,
             tiles,
         ),
-    )
+    ).astype(BF16)
     ffn_grad, ffn_first, ffn_second, ffn_step, ffn_sums = adam(
-        my_slot, gather_group(ffn_mine), ffn_master, ffn_m, ffn_v
+        my_slot, gather_direct(ffn_mine), ffn_master, ffn_m, ffn_v
     )
 
     grad_blocks = grad_attended.reshape(blocks, BLOCK, D)
     glob_part = jnp.sum(
         jnp.where(hits[:, :, None, None], grad_blocks[None], 0), axis=1, dtype=F32
     ).astype(BF16)
-    for mask in all_masks():
+    for mask in all_masks()[:-1]:
         glob_part = glob_part + exchange(glob_part, mask)
-    grad_glob = glob_part.reshape(2 * BLOCK, D)
+    glob_in = exchange(glob_part, all_masks()[-1])
     grad_sparse = jnp.where((hits[0] | hits[1])[:, None, None], 0, grad_blocks).reshape(rows, D)
-    near_dquery, used_grads, near = sparse_bwd(window_nvalid, query, grad_sparse, lse, kv_used)
-    near_dquery, used_grads = global_bwd(
-        chunk_nvalid[:1], glob_query, grad_glob, glob_pairs, kv_used, near, used_grads, near_dquery
-    )
+    near_dquery, used_grads = attention_bwd(
+        jnp.concatenate([window_nvalid, chunk_nvalid[:1]]),
+        query,
+        grad_sparse,
+        lse,
+        kv_used,
+        glob_query,
+        glob_part.reshape(2 * BLOCK, D),
+        glob_in.reshape(2 * BLOCK, D),
+        glob_pairs,
+    )
+    used_grads = used_grads.reshape(-1, 2 * D)
 
     g_query = mm(x_near, near_dquery, TN).astype(BF16)
     g_kv = mm(x_used, used_grads, TN).astype(BF16)
@@ -1129,8 +1080,36 @@
     attn_sent = jnp.where(on_core, early, late)
     attn_keep = jnp.where(on_core, late, early)
     attn_spec = pl.BlockSpec((2, D // tiles, D), lambda t, *a: (0, t, 0))
-    attn_mine = finish(
-        *reduce_group(
+    vec_local = jnp.stack(
+        [
+            jnp.sum(near_dquery, axis=0, dtype=F32),
+            jnp.sum(used_grads[:, D:], axis=0, dtype=F32),
+            jnp.sum(grad_branch, axis=0, dtype=F32),
+            jnp.sum(grad_down, axis=0, dtype=F32),
+            jnp.sum(grad_norm * normal_one, axis=0),
+            jnp.sum(grad_norm, axis=0),
+            jnp.sum(grad_out * normal_two, axis=0),
+            jnp.sum(grad_out, axis=0),
+        ]
+    )
+    bias_local = jnp.sum(grad_upper, axis=0, dtype=F32).reshape(GROUP, CUT)[
+        my_slot ^ relative[:GROUP]
+    ]
+    small_local = jnp.concatenate(
+        [
+            vec_local.reshape(8, wa_count, wide).transpose(1, 0, 2).reshape(wa_count, 8 * wide),
+            bias_local.reshape(wa_count, FF // wa_count),
+        ],
+        axis=1,
+    )
+    small_sum = small_local
+    for mask in all_masks():
+        small_sum = small_sum + exchange(small_sum, mask)
+    small_rows = jnp.pad(small_sum, ((0, 0), (0, 8 * CUT - small_sum.shape[1])))
+    small_rows = small_rows.reshape(wa_count, 8, CUT).astype(BF16)
+
+    attn_total = finish(
+        reduce_group(
             my_slot,
             [attn_keep, exchange(attn_sent, CORE)],
             [attn_spec] * 2,
@@ -1139,9 +1118,14 @@
             read_attn,
             tiles,
         ),
-    )
+        small_rows,
+    )
+    attn_mine = attn_total[:wide].astype(BF16)
+    small_mine = attn_total[wide:].reshape(-1)
+    vec_grad = small_mine[: 8 * wide].reshape(8, wide)
+    bias_grad = small_mine[8 * wide : 8 * wide + FF // wa_count]
     attn_grad, attn_first, attn_second, attn_step, attn_sums = adam(
-        my_slot, gather_group(attn_mine), attn_master, attn_m, attn_v
+        my_slot, gather_direct(attn_mine), attn_master, attn_m, attn_v
     )
 
     dx_used = mm(used_grads, w_kv, NT).astype(BF16)
@@ -1165,47 +1149,21 @@
         read_rows,
         tiles,
     )
-    input_grad = grad_first + jnp.concatenate(dx_own, axis=0)
-
-    vec_local = jnp.stack(
-        [
-            jnp.sum(near_dquery, axis=0, dtype=F32),
-            jnp.sum(used_grads[:, D:], axis=0, dtype=F32),
-            jnp.sum(grad_branch, axis=0, dtype=F32),
-            jnp.sum(grad_down, axis=0, dtype=F32),
-            jnp.sum(grad_norm * normal_one, axis=0),
-            jnp.sum(grad_norm, axis=0),
-            jnp.sum(grad_out * normal_two, axis=0),
-            jnp.sum(grad_out, axis=0),
-        ]
-    )
-    bias_local = jnp.sum(grad_upper, axis=0, dtype=F32).reshape(GROUP, CUT)[
-        my_slot ^ relative[:GROUP]
-    ]
-    small_local = jnp.concatenate(
-        [
-            vec_local.reshape(8, wa_count, wide).transpose(1, 0, 2).reshape(wa_count, 8 * wide),
-            bias_local.reshape(wa_count, FF // wa_count),
-        ],
-        axis=1,
-    )
-    small_sum = wa_reduce(small_local)
-    for mask in all_masks():
-        small_sum = small_sum + exchange(small_sum, mask)
-    vec_grad = small_sum[: 8 * wide].reshape(8, wide)
-    bias_grad = small_sum[8 * wide :]
+    input_grad = grad_first + dx_own
 
     vec_first, vec_second, vec_adam = adam_moments(vec_m, vec_v, vec_grad)
     bias_first, bias_second, bias_adam = adam_moments(bias_m, bias_v, bias_grad)
 
-    def ratio_of(sums):
-        squares = jnp.sqrt(wa_total(jnp.sum(sums, axis=(1, 2))))
-        count = squares.shape[0] // 2
-        return squares[:count], squares[count:], squares[:count] / (squares[count:] + RATIO_EPS)
-
-    ffn_norm, ffn_length, ffn_ratio = ratio_of(ffn_sums)
+    squares = wa_total(
+        jnp.concatenate([jnp.sum(attn_sums, axis=(1, 2)), jnp.sum(ffn_sums, axis=(1, 2))])
+    )
+    squares = jnp.sqrt(squares)
+    attn_norm, attn_length, ffn_norm, ffn_length = (
+        squares[:4], squares[4:8], squares[8:10], squares[10:]
+    )
+    attn_ratio = attn_norm / (attn_length + RATIO_EPS)
+    ffn_ratio = ffn_norm / (ffn_length + RATIO_EPS)
     ffn_new, ffn_copy = final(ffn_ratio, ffn_master, ffn_step)
-    attn_norm, attn_length, attn_ratio = ratio_of(attn_sums)
     attn_new, attn_copy = final(attn_ratio, attn_master, attn_step)
     ratios = jnp.concatenate([attn_ratio, ffn_ratio])
     norms = jnp.stack(

time: 514 us -> 519 us (level)
  waiting for transfers between devices: 147 us -> 171 us
  Pallas kernels: 141 us -> 133 us
  starting transfers between devices: 83.5 us -> 77.9 us
    ppermute x70 -> x63, waiting for transfers between devices: 102 us -> 138 us  [exchange(): return lax.ppermute(value, CTX, [(i, i ^ mask) for i in range(count)])]
    ppermute x21 -> x12, waiting for transfers between devices: 44.7 us -> 25.5 us  [wa_shift(): lax.ppermute(value, WA, [(i, (i + step) % count) for i in range(count)])]
    ppermute x0 -> x2, waiting for transfers between devices: none -> 8.02 us  [wa_total(): value = value + lax.ppermute(value, WA, pairs)]
    ppermute x21 -> x12, starting transfers between devices: 34 us -> 29.8 us  [wa_shift(): lax.ppermute(value, WA, [(i, (i + step) % count) for i in range(count)])]
    pallas_call x2 -> x1, Pallas kernels: 31.6 us -> 28.1 us  [attention_bwd(): pl.pallas_call(attention_bwd_kernel, grid_spec=pltpu.PrefetchScalarGridSp...]
    ppermute x70 -> x63, starting transfers between devices: 49.5 us -> 48.1 us  [exchange(): return lax.ppermute(value, CTX, [(i, i ^ mask) for i in range(count)])]
    unnamed x159 -> x162, local copies, waits for them, and re-layouts: 11.4 us -> 10.7 us
  transfers between devices with their start and end apart: 91 -> 77, of which waited for: 28 -> 27; matrix products, arithmetic and copies ran while one was open for 18% -> 19% of each run, Pallas kernels for 17% -> 19%
where the time goes in v1:
time: 519 us; the launch traced here: 514 us
  waiting for transfers between devices  171 us (33%)
  Pallas kernels  133 us (26%)
  starting transfers between devices  77.9 us (15%)
  other arithmetic  49.3 us (9%)
  matrix products  47.8 us (9%)
  local copies, waits for them, and re-layouts  30.5 us (6%)
    ppermute x63, waiting for transfers between devices, exchange(): return lax.ppermute(value, CTX, [(i, i ^ mask) for i in range(count)])  138 us
    ppermute x63, starting transfers between devices, exchange(): return lax.ppermute(value, CTX, [(i, i ^ mask) for i in range(count)])  48.1 us
    dot_general x15, matrix products, mm(): return lax.dot_general(a, b, dims, preferred_element_type=F32)  47.8 us
    ppermute x12, starting transfers between devices, wa_shift(): lax.ppermute(value, WA, [(i, (i + step) % count) for i in range(count)])  29.8 us
    pallas_call x1, Pallas kernels, attention_bwd(): pl.pallas_call(attention_bwd_kernel, grid_spec=pltpu.PrefetchScalarGridSp...  28.1 us
    ppermute x12, waiting for transfers between devices, wa_shift(): lax.ppermute(value, WA, [(i, (i + step) % count) for i in range(count)])  25.5 us
    pallas_call x2, Pallas kernels, adam(): pl.pallas_call(functools.partial(adam_kernel, pieces=piece_columns // CUT...  18.6 us
    pallas_call x3, Pallas kernels, spread(): pl.pallas_call(functools.partial(spread_kernel, read=read), grid_spec=plt...  15.5 us
  transfers between devices with their start and end apart: 77, of which 27 were waited for; matrix products, arithmetic and copies ran while one was open for 19% of the time, Pallas kernels for 19%

profile of v1, /device:TPU:0, one launch (start us, length us, event | category | flops | bytes accessed | tf_op | source)
XLA Modules:
  0.0 514.0 jit_solution(5076514166754943950)
XLA Ops:
  0.7 3.0 collective-permute-start.3
  10.1 2.6 collective-permute-start.6
  16.7 4.7 collective-permute-done.3.refs_1_
  24.0 2.6 collective-permute-start.1
  36.7 8.4 %collective-permute-done.8.refs_1_ = bf16[768,384]{1,0:T(8,128)(2,1)S(1)} collective-permute-done((bf16[768,384]{1,0:T(8,128)(2,1)}, bf16[768,384]{1,0:T(8,128)(2,1)S(1)}, u32[]{:S(2)}, u32[]{:S(2)}) %collective-permute-start.8) | collective-permute-done | bytes 589856 | tf_op jit(solution)/shard_map/ppermute | solution.py:474
  52.4 4.8 collective-permute-done.17.refs_3_
  74.3 5.6 %aw.1 = (bf16[768,768]{1,0:T(8,128)(2,1)}, bf16[768,1536]{1,0:T(8,128)(2,1)}, bf16[768,768]{1,0:T(8,128)(2,1)}) custom-call(s32[1]{0:T(128)} %bitcast.5.where_ref.slot_ref, bf16[768,384]{1,0:T(8,128)(2,1)} %get-tuple-element.84.refs_0_, bf16[768,384]{1,0:T(8,128)(2,1)} %copy-done.7, bf16[768,384]{1,0:T(8,128)(2,1)} %copy-done.8, ...), custom_call_target="tpu_custom_call" | custom-call | bytes 9437184 | tf_op jit(solution)/shard_map/aw/pallas_call | solution.py:668
  80.0 11.8 %kv.1 = (bf16[2304,1536]{1,0:T(8,128)(2,1)}, bf16[2304,768]{1,0:T(8,128)(2,1)}) custom-call(s32[11]{0:T(128)} %convert_reduce_fusion.6.start_ref, s32[36]{0:T(128)} %get-tuple-element.149.order_ref, s32[36]{0:T(128)} %get-tuple-element.148.index_ref, bf16[768,1536]{1,0:T(8,128)(2,1)} %get-tuple-element.86.w_ref.k_ref.v_ref, ...), custom_call_target="tpu_custom_call" | custom-call | flops 5435817984 | bytes 14155776 | tf_op jit(solution)/shard_map/kv/pallas_call | solution.py:430
  93.8 11.1 %gf.1 = f32[136,128]{1,0:T(8,128)} custom-call(s32[1]{0:T(128)} %bitcast.3.pair_ref, s32[8]{0:T(128)} %fusion.58.nvalid_ref, bf16[128,768]{1,0:T(8,128)(2,1)} %fusion.21.q_ref.gq_ref, bf16[768,1536]{1,0:T(8,128)(2,1)} %get-tuple-element.86.w_ref.k_ref.v_ref, bf16[768,1536]{1,0:T(8,128)(2,1)} %get-tuple-element.86.w_ref.k_ref.v_ref, ...), custom_call_target="tpu_custom_call" | custom-call | flops 1879048192 | bytes 6291456 | tf_op jit(solution)/shard_map/gf/pallas_call | solution.py:386
  115.3 2.3 join.3
  121.7 14.8 %sf.1 = (bf16[512,768]{1,0:T(8,128)(2,1)}, f32[8,8,256]{2,1,0:T(8,128)}) custom-call(s32[24]{0:T(128)} %select_n.374.nvalid_ref, bf16[512,768]{1,0:T(8,128)(2,1)} %fusion.18.q_ref, bf16[36,64,1536]{2,1,0:T(8,128)(2,1)} %bitcast.131, bf16[36,64,1536]{2,1,0:T(8,128)(2,1)} %bitcast.132), custom_call_target="tpu_custom_call" | custom-call | flops 805306368 | bytes 12582912 | tf_op jit(solution)/shard_map/sf/pallas_call | solution.py:315
  137.9 7.2 %collective-permute-done.27.refs_1_ = bf16[768,768]{1,0:T(8,128)(2,1)} collective-permute-done((bf16[768,768]{1,0:T(8,128)(2,1)}, bf16[768,768]{1,0:T(8,128)(2,1)}, u32[]{:S(2)}, u32[]{:S(2)}) %collective-permute-start.27) | collective-permute-done | bytes 1179680 | tf_op jit(solution)/shard_map/ppermute | solution.py:474
  150.9 9.0 %collective-permute-done.29.refs_3_ = bf16[384,768]{1,0:T(8,128)(2,1)S(1)} collective-permute-done((bf16[384,768]{1,0:T(8,128)(2,1)S(1)}, bf16[384,768]{1,0:T(8,128)(2,1)S(1)}, u32[]{:S(2)}, u32[]{:S(2)}) %collective-permute-start.29) | collective-permute-done | bytes 589856 | tf_op jit(solution)/shard_map/ppermute | solution.py:474
  165.6 14.7 %ff.1 = (bf16[512,3072]{1,0:T(8,128)(2,1)}, bf16[512,3072]{1,0:T(8,128)(2,1)}, f32[512,768]{1,0:T(8,128)}, bf16[768,3072]{1,0:T(8,128)(2,1)}, bf16[768,3072]{1,0:T(8,128)(2,1)}) custom-call(bf16[512,768]{1,0:T(8,128)(2,1)} %fusion.16.n_ref, f32[4,1,768]{2,1,0:T(1,128)} %reshape.683.b_ref, bf16[768,768]{1,0:T(8,128)(2,1)} %get-tuple-element.99.refs_0_, ...), custom_call_target="tpu_custom_call" | custom-call | flops 4831838208 | bytes 15728640 | tf_op jit(solution)/shard_map/ff/pallas_call | solution.py:753
  186.2 3.2 convert_reduce_fusion.1
  189.4 3.4 multiply_reduce_fusion
  197.8 4.4 convolution_convert_fusion.3
  203.6 2.8 convolution_convert_fusion.2
  206.6 3.0 collective-permute-done.37
  212.0 4.1 collective-permute-done.38
  216.8 28.1 %sb.1 = (bf16[768,768]{1,0:T(8,128)(2,1)}, bf16[36,64,1536]{2,1,0:T(8,128)(2,1)}) custom-call(s32[25]{0:T(128)} %pad_add_fusion.1.nvalid_ref, bf16[512,768]{1,0:T(8,128)(2,1)} %fusion.18.q_ref, bf16[512,768]{1,0:T(8,128)(2,1)} %get-tuple-element.206.do_ref, f32[8,8,256]{2,1,0:T(8,128)} %get-tuple-element.104.lse_ref, bf16[36,64,1536]{2,1,0:T(8,128)(2,1)} %bitcast.133, ...), custom_call_target="tpu_custom_call" | custom-call | flops 2516582400 | bytes 25165824 | tf_op jit(solution)/shard_map/sb/pallas_call | solution.py:348
  245.0 9.2 %convolution_convert_fusion.1 = bf16[768,1536]{1,0:T(8,128)(2,1)S(1)} fusion(bf16[2304,768]{1,0:T(8,128)(2,1)} %get-tuple-element.90, bf16[2304,1536]{1,0:T(8,128)(2,1)} %bitcast.142), kind=kOutput, calls=%fused_computation.7 | convolution fusion | flops 5436997632 | bytes 12976128 | tf_op jit(solution)/shard_map/dot_general | solution.py:44
  255.6 2.6 broadcast_select_fusion
  259.9 7.1 %convolution_convert_fusion = bf16[2304,768]{1,0:T(8,128)(2,1)} fusion(bf16[2304,1536]{1,0:T(8,128)(2,1)S(1)} %bitcast.146, bf16[768,1536]{1,0:T(8,128)(2,1)S(1)} %copy-done), kind=kOutput, calls=%fused_computation.5 | convolution fusion | flops 5437587456 | bytes 12976128 | tf_op jit(solution)/shard_map/dot_general | solution.py:44
  269.1 6.5 %pb.1 = (bf16[32,64,768]{2,1,0:T(8,128)(2,1)}, bf16[32,64,768]{2,1,0:T(8,128)(2,1)}) custom-call(s32[36]{0:T(128)} %get-tuple-element.175.table_ref, bf16[36,64,768]{2,1,0:T(8,128)(2,1)} %bitcast.139, bf16[12,64,768]{2,1,0:T(8,128)(2,1)} %bitcast.147), custom_call_target="tpu_custom_call" | custom-call | bytes 13369344 | tf_op jit(solution)/shard_map/pb/pallas_call | solution.py:457
  276.0 2.6 convert_reduce_fusion
  279.4 2.3 collective-permute-done.47
  283.0 4.6 shard_map.353
  289.9 4.5 convolution_convert_fusion.5.refs_0_
  295.7 2.8 convolution_convert_fusion.4.refs_1_
  298.5 6.0 %shard_map.355 = (bf16[768,768]{1,0:T(8,128)(2,1)}, bf16[768,768]{1,0:T(8,128)(2,1)}, bf16[768,768]{1,0:T(8,128)(2,1)}, bf16[768,768]{1,0:T(8,128)(2,1)}) custom-call(s32[1]{0:T(128)} %bitcast.5.where_ref.slot_ref, bf16[768,1536]{1,0:T(8,128)(2,1)} %convolution_convert_fusion.5.refs_0_, bf16[768,1536]{1,0:T(8,128)(2,1)} %convolution_convert_fusion.4.refs_1_, ...), custom_call_target="tpu_custom_call" | custom-call | bytes 14155776 | tf_op jit(solution)/shard_map/pallas_call | solution.py:796
  306.0 36.6 %collective-permute-done.49 = f32[4,2304]{1,0:T(4,128)S(1)} collective-permute-done((f32[4,2304]{1,0:T(4,128)S(1)}, f32[4,2304]{1,0:T(4,128)S(1)}, u32[]{:S(2)}, u32[]{:S(2)}) %collective-permute-start.49) | collective-permute-done | bytes 36896 | tf_op jit(solution)/shard_map/ppermute | solution.py:474
  345.7 38.4 %collective-permute-done.44 = bf16[768,384]{1,0:T(8,128)(2,1)S(1)} collective-permute-done((bf16[768,384]{1,0:T(8,128)(2,1)}, bf16[768,384]{1,0:T(8,128)(2,1)S(1)}, u32[]{:S(2)}, u32[]{:S(2)}) %collective-permute-start.44) | collective-permute-done | bytes 589856 | tf_op jit(solution)/shard_map/ppermute | solution.py:474
  386.7 12.9 %collective-permute-start.51 = (bf16[200,384]{1,0:T(8,128)(2,1)S(1)}, bf16[200,384]{1,0:T(8,128)(2,1)}, u32[]{:S(2)}, u32[]{:S(2)}) collective-permute-start(bf16[200,384]{1,0:T(8,128)(2,1)S(1)} %get-tuple-element.185), channel_id=1, source_target_pairs={{0,2},{1,3},{2,0},{3,1},{4,6},{5,7},{6,4},{7,5},{8,10},{9,11},{10,... | collective-permute-start | bytes 460808 | tf_op jit(solution)/shard_map/ppermute | solution.py:495
  399.7 2.6 add_convert_fusion
  403.3 3.8 collective-permute-start.67
  408.8 6.5 %collective-permute-done.51 = bf16[200,384]{1,0:T(8,128)(2,1)} collective-permute-done((bf16[200,384]{1,0:T(8,128)(2,1)S(1)}, bf16[200,384]{1,0:T(8,128)(2,1)}, u32[]{:S(2)}, u32[]{:S(2)}) %collective-permute-start.51) | collective-permute-done | bytes 153632 | tf_op jit(solution)/shard_map/ppermute | solution.py:495
  418.6 19.0 %collective-permute-done.66 = bf16[192,768]{1,0:T(8,128)(2,1)} collective-permute-done((bf16[192,768]{1,0:T(8,128)(2,1)}, bf16[192,768]{1,0:T(8,128)(2,1)}, u32[]{:S(2)}, u32[]{:S(2)}) %collective-permute-start.66) | collective-permute-done | bytes 294944 | tf_op jit(solution)/shard_map/ppermute | solution.py:495
  446.6 4.6 collective-permute-done.68.refs_1_
  451.3 3.6 collective-permute-done.69.refs_2_
  460.4 4.9 shard_map.352
  467.8 6.8 %shard_map.354 = (f32[4,192,768]{2,1,0:T(8,128)}, f32[4,192,768]{2,1,0:T(8,128)}, f32[4,192,768]{2,1,0:T(8,128)}, bf16[4,192,768]{2,1,0:T(8,128)(2,1)}, f32[8,8,768]{2,1,0:T(8,128)}) custom-call(s32[1]{0:T(128)} %bitcast.5.where_ref.slot_ref, bf16[192,384]{1,0:T(8,128)(2,1)} %copy-done.31, bf16[192,384]{1,0:T(8,128)(2,1)} %copy-done.40, ...), custom_call_target="tpu_custom_call" | custom-call | flops 11796480 | bytes 17694720 | tf_op jit(solution)/shard_map/pallas_call | solution.py:862
  477.6 11.8 %shard_map.356 = (f32[2,192,3072]{2,1,0:T(8,128)}, f32[2,192,3072]{2,1,0:T(8,128)}, f32[2,192,3072]{2,1,0:T(8,128)}, bf16[2,192,3072]{2,1,0:T(8,128)(2,1)}, f32[4,8,3072]{2,1,0:T(8,128)}) custom-call(s32[1]{0:T(128)} %bitcast.5.where_ref.slot_ref, bf16[192,768]{1,0:T(8,128)(2,1)} %copy-done.18, bf16[192,768]{1,0:T(8,128)(2,1)} %copy-done.34, ...), custom_call_target="tpu_custom_call" | custom-call | flops 23592960 | bytes 35389440 | tf_op jit(solution)/shard_map/pallas_call | solution.py:862
  490.6 3.6 collective-permute-done.75
  494.3 4.5 collective-permute-done.76
  498.9 4.0 fusion.73
  504.2 6.6 %fusion.72 = (bf16[2,192,3072]{2,1,0:T(8,128)(2,1)}, f32[2,192,3072]{2,1,0:T(8,128)}) fusion(f32[2,192,3072]{2,1,0:T(8,128)} %refs_8_.3, bf16[2,192,3072]{2,1,0:T(8,128)(2,1)S(1)} %copy-done.4, f32[2]{0:T(128)S(1)} %get-tuple-element.162), kind=kLoop, calls=%fused_computation.243 | loop fusion | flops 4718592 | bytes 14155784 | tf_op jit(solution)/shard_map/convert_element_type | solution.py:852
  510.8 3.0 add_bitcast_fusion
  (426 shorter events, 136.9 us)
Async XLA Ops:
  0.7 20.8 %collective-permute-start.3 = (bf16[512,768]{1,0:T(8,128)(2,1)}, bf16[512,768]{1,0:T(8,128)(2,1)S(1)}, u32[]{:S(2)}, u32[]{:S(2)}) collective-permute-start(bf16[512,768]{1,0:T(8,128)(2,1)} %bitcast.149), channel_id=1, source_target_pairs={{0,8},{4,12},{8,0},{12,4},{16,24},{20,28},{24,16},{28,20},{1,9},{5... | collective-permute-start | bytes 2359304 | tf_op jit(solution)/shard_map/ppermute | solution.py:474
  3.7 20.4 %collective-permute-start.4 = (bf16[512,768]{1,0:T(8,128)(2,1)}, bf16[512,768]{1,0:T(8,128)(2,1)S(1)}, u32[]{:S(2)}, u32[]{:S(2)}) collective-permute-start(bf16[512,768]{1,0:T(8,128)(2,1)} %bitcast.150), channel_id=1, source_target_pairs={{0,16},{4,20},{8,24},{12,28},{16,0},{20,4},{24,8},{28,12},{1,17},{... | collective-permute-start | bytes 2359304 | tf_op jit(solution)/shard_map/ppermute | solution.py:474
  8.5 18.9 %collective-permute-start.5 = (bf16[208,384]{1,0:T(8,128)(2,1)}, bf16[208,384]{1,0:T(8,128)(2,1)S(1)}, u32[]{:S(2)}, u32[]{:S(2)}) collective-permute-start(bf16[208,384]{1,0:T(8,128)(2,1)} %get-tuple-element.80.refs_0_), channel_id=1, source_target_pairs={{0,1},{1,2},{2,3},{3,0},{4,5},{5,6},{6,7},{7,4},{8,9},{9,10},{10,1... | collective-permute-start | bytes 479240 | tf_op jit(solution)/shard_map/ppermute | solution.py:495
  10.1 18.7 %collective-permute-start.6 = (bf16[208,384]{1,0:T(8,128)(2,1)}, bf16[208,384]{1,0:T(8,128)(2,1)S(1)}, u32[]{:S(2)}, u32[]{:S(2)}) collective-permute-start(bf16[208,384]{1,0:T(8,128)(2,1)} %get-tuple-element.80.refs_0_), channel_id=1, source_target_pairs={{0,2},{1,3},{2,0},{3,1},{4,6},{5,7},{6,4},{7,5},{8,10},{9,11},{10,... | collective-permute-start | bytes 479240 | tf_op jit(solution)/shard_map/ppermute | solution.py:495
  12.7 16.1 %collective-permute-start.7 = (bf16[208,384]{1,0:T(8,128)(2,1)}, bf16[208,384]{1,0:T(8,128)(2,1)S(1)}, u32[]{:S(2)}, u32[]{:S(2)}) collective-permute-start(bf16[208,384]{1,0:T(8,128)(2,1)} %get-tuple-element.80.refs_0_), channel_id=1, source_target_pairs={{0,3},{1,0},{2,1},{3,2},{4,7},{5,4},{6,5},{7,6},{8,11},{9,8},{10,9... | collective-permute-start | bytes 479240 | tf_op jit(solution)/shard_map/ppermute | solution.py:495
  21.4 26.7 %collective-permute-start = (bf16[192,768]{1,0:T(8,128)(2,1)}, bf16[192,768]{1,0:T(8,128)(2,1)}, u32[]{:S(2)}, u32[]{:S(2)}) collective-permute-start(bf16[192,768]{1,0:T(8,128)(2,1)} %get-tuple-element.95.refs_0_), channel_id=1, source_target_pairs={{0,1},{1,2},{2,3},{3,0},{4,5},{5,6},{6,7},{7,4},{8,9},{9,10},{10,1... | collective-permute-start | bytes 884744 | tf_op jit(solution)/shard_map/ppermute | solution.py:495
  24.0 24.2 %collective-permute-start.1 = (bf16[192,768]{1,0:T(8,128)(2,1)}, bf16[192,768]{1,0:T(8,128)(2,1)}, u32[]{:S(2)}, u32[]{:S(2)}) collective-permute-start(bf16[192,768]{1,0:T(8,128)(2,1)} %get-tuple-element.95.refs_0_), channel_id=1, source_target_pairs={{0,2},{1,3},{2,0},{3,1},{4,6},{5,7},{6,4},{7,5},{8,10},{9,11},{10,... | collective-permute-start | bytes 884744 | tf_op jit(solution)/shard_map/ppermute | solution.py:495
  27.4 21.7 %collective-permute-start.2 = (bf16[192,768]{1,0:T(8,128)(2,1)}, bf16[192,768]{1,0:T(8,128)(2,1)}, u32[]{:S(2)}, u32[]{:S(2)}) collective-permute-start(bf16[192,768]{1,0:T(8,128)(2,1)} %get-tuple-element.95.refs_0_), channel_id=1, source_target_pairs={{0,3},{1,0},{2,1},{3,2},{4,7},{5,4},{6,5},{7,6},{8,11},{9,8},{10,9... | collective-permute-start | bytes 884744 | tf_op jit(solution)/shard_map/ppermute | solution.py:495
  33.0 14.3 %collective-permute-start.9 = (bf16[768,384]{1,0:T(8,128)(2,1)}, bf16[768,384]{1,0:T(8,128)(2,1)S(1)}, u32[]{:S(2)}, u32[]{:S(2)}) collective-permute-start(bf16[768,384]{1,0:T(8,128)(2,1)} %get-tuple-element.84.refs_0_), channel_id=1, source_target_pairs={{0,16},{4,20},{8,24},{12,28},{16,0},{20,4},{24,8},{28,12},{1,17},{... | collective-permute-start | bytes 1769480 | tf_op jit(solution)/shard_map/ppermute | solution.py:474
  48.2 14.1 %collective-permute-start.12 = (bf16[768,384]{1,0:T(8,128)(2,1)}, bf16[768,384]{1,0:T(8,128)(2,1)}, u32[]{:S(2)}, u32[]{:S(2)}) collective-permute-start(bf16[768,384]{1,0:T(8,128)(2,1)} %get-tuple-element.84.refs_0_), channel_id=1, source_target_pairs={{0,4},{4,0},{8,12},{12,8},{16,20},{20,16},{24,28},{28,24},{1,5},{5... | collective-permute-start | bytes 1769480 | tf_op jit(solution)/shard_map/ppermute | solution.py:474
  62.3 17.6 %collective-permute-start.19 = (bf16[512,768]{1,0:T(8,128)(2,1)S(1)}, bf16[512,768]{1,0:T(8,128)(2,1)}, u32[]{:S(2)}, u32[]{:S(2)}) collective-permute-start(bf16[512,768]{1,0:T(8,128)(2,1)S(1)} %bitcast.153), channel_id=1, source_target_pairs={{0,4},{4,0},{8,12},{12,8},{16,20},{20,16},{24,28},{28,24},{1,5},{5... | collective-permute-start | bytes 2359304 | tf_op jit(solution)/shard_map/ppermute | solution.py:474
  63.1 16.8 %collective-permute-start.20 = (bf16[512,768]{1,0:T(8,128)(2,1)S(1)}, bf16[512,768]{1,0:T(8,128)(2,1)}, u32[]{:S(2)}, u32[]{:S(2)}) collective-permute-start(bf16[512,768]{1,0:T(8,128)(2,1)S(1)} %collective-permute-done.3.refs_1_), channel_id=1, source_target_pairs={{0,4},{4,0},{8,12},{12,8},{16,20},{20,16},{24,28},{28,24},{1,5},{5... | collective-permute-start | bytes 2359304 | tf_op jit(solution)/shard_map/ppermute | solution.py:474
  63.7 16.3 %collective-permute-start.21 = (bf16[512,768]{1,0:T(8,128)(2,1)S(1)}, bf16[512,768]{1,0:T(8,128)(2,1)}, u32[]{:S(2)}, u32[]{:S(2)}) collective-permute-start(bf16[512,768]{1,0:T(8,128)(2,1)S(1)} %collective-permute-done.4.refs_2_), channel_id=1, source_target_pairs={{0,4},{4,0},{8,12},{12,8},{16,20},{20,16},{24,28},{28,24},{1,5},{5... | collective-permute-start | bytes 2359304 | tf_op jit(solution)/shard_map/ppermute | solution.py:474
  64.3 15.6 %collective-permute-start.22 = (bf16[256,768]{1,0:T(8,128)(2,1)}, bf16[256,768]{1,0:T(8,128)(2,1)}, u32[]{:S(2)}, u32[]{:S(2)}) collective-permute-start(bf16[256,768]{1,0:T(8,128)(2,1)} %copy-done.32), channel_id=1, source_target_pairs={{0,4},{4,0},{8,12},{12,8},{16,20},{20,16},{24,28},{28,24},{1,5},{5... | collective-permute-start | bytes 1179656 | tf_op jit(solution)/shard_map/ppermute | solution.py:474
  64.7 15.3 %collective-permute-start.23 = (bf16[256,768]{1,0:T(8,128)(2,1)}, bf16[256,768]{1,0:T(8,128)(2,1)}, u32[]{:S(2)}, u32[]{:S(2)}) collective-permute-start(bf16[256,768]{1,0:T(8,128)(2,1)} %copy-done.33), channel_id=1, source_target_pairs={{0,4},{4,0},{8,12},{12,8},{16,20},{20,16},{24,28},{28,24},{1,5},{5... | collective-permute-start | bytes 1179656 | tf_op jit(solution)/shard_map/ppermute | solution.py:474
  117.7 27.4 %collective-permute-start.27 = (bf16[768,768]{1,0:T(8,128)(2,1)}, bf16[768,768]{1,0:T(8,128)(2,1)}, u32[]{:S(2)}, u32[]{:S(2)}) collective-permute-start(bf16[768,768]{1,0:T(8,128)(2,1)} %get-tuple-element.99.refs_0_), channel_id=1, source_target_pairs={{0,8},{4,12},{8,0},{12,4},{16,24},{20,28},{24,16},{28,20},{1,9},{5... | collective-permute-start | bytes 3538952 | tf_op jit(solution)/shard_map/ppermute | solution.py:474
  118.0 28.6 %collective-permute-start.28 = (bf16[768,768]{1,0:T(8,128)(2,1)}, bf16[768,768]{1,0:T(8,128)(2,1)}, u32[]{:S(2)}, u32[]{:S(2)}) collective-permute-start(bf16[768,768]{1,0:T(8,128)(2,1)} %get-tuple-element.99.refs_0_), channel_id=1, source_target_pairs={{0,16},{4,20},{8,24},{12,28},{16,0},{20,4},{24,8},{28,12},{1,17},{... | collective-permute-start | bytes 3538952 | tf_op jit(solution)/shard_map/ppermute | solution.py:474
  119.4 44.2 %collective-permute-start.31 = (bf16[768,768]{1,0:T(8,128)(2,1)}, bf16[768,768]{1,0:T(8,128)(2,1)}, u32[]{:S(2)}, u32[]{:S(2)}) collective-permute-start(bf16[768,768]{1,0:T(8,128)(2,1)} %get-tuple-element.99.refs_0_), channel_id=1, source_target_pairs={{0,4},{4,0},{8,12},{12,8},{16,20},{20,16},{24,28},{28,24},{1,5},{5... | collective-permute-start | bytes 3538952 | tf_op jit(solution)/shard_map/ppermute | solution.py:474
  119.4 17.1 %collective-permute-start.26 = (f32[4,136,128]{2,1,0:T(8,128)S(1)}, f32[4,136,128]{2,1,0:T(8,128)S(1)}, u32[]{:S(2)}, u32[]{:S(2)}) collective-permute-start(f32[4,136,128]{2,1,0:T(8,128)S(1)} %pad_maximum_fusion.3), channel_id=1, source_target_pairs={{0,4},{4,0},{8,12},{12,8},{16,20},{20,16},{24,28},{28,24},{1,5},{5... | collective-permute-start | bytes 835592 | tf_op jit(solution)/shard_map/ppermute | solution.py:474
  147.7 13.7 %collective-permute-start.30 = (bf16[384,768]{1,0:T(8,128)(2,1)S(1)}, bf16[384,768]{1,0:T(8,128)(2,1)S(1)}, u32[]{:S(2)}, u32[]{:S(2)}) collective-permute-start(bf16[384,768]{1,0:T(8,128)(2,1)S(1)} %slice.207), channel_id=1, source_target_pairs={{0,8},{4,12},{8,0},{12,4},{16,24},{20,28},{24,16},{28,20},{1,9},{5... | collective-permute-start | bytes 1769480 | tf_op jit(solution)/shard_map/ppermute | solution.py:474
  149.2 14.4 %collective-permute-start.32 = (bf16[768,768]{1,0:T(8,128)(2,1)}, bf16[768,768]{1,0:T(8,128)(2,1)S(1)}, u32[]{:S(2)}, u32[]{:S(2)}) collective-permute-start(bf16[768,768]{1,0:T(8,128)(2,1)} %collective-permute-done.27.refs_1_), channel_id=1, source_target_pairs={{0,4},{4,0},{8,12},{12,8},{16,20},{20,16},{24,28},{28,24},{1,5},{5... | collective-permute-start | bytes 3538952 | tf_op jit(solution)/shard_map/ppermute | solution.py:474
  149.2 15.4 %collective-permute-start.33 = (bf16[768,768]{1,0:T(8,128)(2,1)}, bf16[768,768]{1,0:T(8,128)(2,1)}, u32[]{:S(2)}, u32[]{:S(2)}) collective-permute-start(bf16[768,768]{1,0:T(8,128)(2,1)} %collective-permute-done.28.refs_2_), channel_id=1, source_target_pairs={{0,4},{4,0},{8,12},{12,8},{16,20},{20,16},{24,28},{28,24},{1,5},{5... | collective-permute-start | bytes 3538952 | tf_op jit(solution)/shard_map/ppermute | solution.py:474
  202.2 92.3 %collective-permute-start.60 = (bf16[768,1536]{1,0:T(8,128)(2,1)}, bf16[768,1536]{1,0:T(8,128)(2,1)}, u32[]{:S(2)}, u32[]{:S(2)}) collective-permute-start(bf16[768,1536]{1,0:T(8,128)(2,1)} %convolution_convert_fusion.3), channel_id=1, source_target_pairs={{0,4},{4,0},{8,12},{12,8},{16,20},{20,16},{24,28},{28,24},{1,5},{5... | collective-permute-start | bytes 7077896 | tf_op jit(solution)/shard_map/ppermute | solution.py:474
  206.4 92.1 %collective-permute-start.61 = (bf16[768,1536]{1,0:T(8,128)(2,1)}, bf16[768,1536]{1,0:T(8,128)(2,1)}, u32[]{:S(2)}, u32[]{:S(2)}) collective-permute-start(bf16[768,1536]{1,0:T(8,128)(2,1)} %convolution_convert_fusion.2), channel_id=1, source_target_pairs={{0,4},{4,0},{8,12},{12,8},{16,20},{20,16},{24,28},{28,24},{1,5},{5... | collective-permute-start | bytes 7077896 | tf_op jit(solution)/shard_map/ppermute | solution.py:474
  258.2 24.8 %collective-permute-start.43 = (bf16[2,768,768]{2,1,0:T(8,128)(2,1)}, bf16[2,768,768]{2,1,0:T(8,128)(2,1)}, u32[]{:S(2)}, u32[]{:S(2)}) collective-permute-start(bf16[2,768,768]{2,1,0:T(8,128)(2,1)} %get-tuple-element.176), channel_id=1, source_target_pairs={{0,4},{4,0},{8,12},{12,8},{16,20},{20,16},{24,28},{28,24},{1,5},{5... | collective-permute-start | bytes 7077896 | tf_op jit(solution)/shard_map/ppermute | solution.py:474
  275.7 166.0 %collective-permute-start.39 = (bf16[32,64,768]{2,1,0:T(8,128)(2,1)}, bf16[32,64,768]{2,1,0:T(8,128)(2,1)}, u32[]{:S(2)}, u32[]{:S(2)}) collective-permute-start(bf16[32,64,768]{2,1,0:T(8,128)(2,1)} %get-tuple-element.108), channel_id=1, source_target_pairs={{0,4},{4,0},{8,12},{12,8},{16,20},{20,16},{24,28},{28,24},{1,5},{5... | collective-permute-start | bytes 9437192 | tf_op jit(solution)/shard_map/ppermute | solution.py:474
  287.6 56.0 %collective-permute-start.46 = (bf16[768,384]{1,0:T(8,128)(2,1)}, bf16[768,384]{1,0:T(8,128)(2,1)}, u32[]{:S(2)}, u32[]{:S(2)}) collective-permute-start(bf16[768,384]{1,0:T(8,128)(2,1)} %get-tuple-element.116), channel_id=1, source_target_pairs={{0,24},{4,28},{8,16},{12,20},{16,8},{20,12},{24,0},{28,4},{1,25},{... | collective-permute-start | bytes 1769480 | tf_op jit(solution)/shard_map/ppermute | solution.py:474
  289.3 55.5 %collective-permute-start.45 = (bf16[768,384]{1,0:T(8,128)(2,1)}, bf16[768,384]{1,0:T(8,128)(2,1)}, u32[]{:S(2)}, u32[]{:S(2)}) collective-permute-start(bf16[768,384]{1,0:T(8,128)(2,1)} %get-tuple-element.115), channel_id=1, source_target_pairs={{0,16},{4,20},{8,24},{12,28},{16,0},{20,4},{24,8},{28,12},{1,17},{... | collective-permute-start | bytes 1769480 | tf_op jit(solution)/shard_map/ppermute | solution.py:474
  294.4 48.1 %collective-permute-start.49 = (f32[4,2304]{1,0:T(4,128)S(1)}, f32[4,2304]{1,0:T(4,128)S(1)}, u32[]{:S(2)}, u32[]{:S(2)}) collective-permute-start(f32[4,2304]{1,0:T(4,128)S(1)} %add.606), channel_id=1, source_target_pairs={{0,16},{4,20},{8,24},{12,28},{16,0},{20,4},{24,8},{28,12},{1,17},{... | collective-permute-start | bytes 110600 | tf_op jit(solution)/shard_map/ppermute | solution.py:474
  304.5 82.2 %collective-permute-start.64 = (bf16[768,768]{1,0:T(8,128)(2,1)}, bf16[768,768]{1,0:T(8,128)(2,1)S(1)}, u32[]{:S(2)}, u32[]{:S(2)}) collective-permute-start(bf16[768,768]{1,0:T(8,128)(2,1)} %get-tuple-element.122), channel_id=1, source_target_pairs={{0,24},{4,28},{8,16},{12,20},{16,8},{20,12},{24,0},{28,4},{1,25},{... | collective-permute-start | bytes 3538952 | tf_op jit(solution)/shard_map/ppermute | solution.py:474
  342.5 57.1 %collective-permute-start.63 = (bf16[768,768]{1,0:T(8,128)(2,1)}, bf16[768,768]{1,0:T(8,128)(2,1)}, u32[]{:S(2)}, u32[]{:S(2)}) collective-permute-start(bf16[768,768]{1,0:T(8,128)(2,1)} %get-tuple-element.121), channel_id=1, source_target_pairs={{0,16},{4,20},{8,24},{12,28},{16,0},{20,4},{24,8},{28,12},{1,17},{... | collective-permute-start | bytes 3538952 | tf_op jit(solution)/shard_map/ppermute | solution.py:474
  343.6 56.0 %collective-permute-start.62 = (bf16[768,768]{1,0:T(8,128)(2,1)}, bf16[768,768]{1,0:T(8,128)(2,1)}, u32[]{:S(2)}, u32[]{:S(2)}) collective-permute-start(bf16[768,768]{1,0:T(8,128)(2,1)} %get-tuple-element.120), channel_id=1, source_target_pairs={{0,8},{4,12},{8,0},{12,4},{16,24},{20,28},{24,16},{28,20},{1,9},{5... | collective-permute-start | bytes 3538952 | tf_op jit(solution)/shard_map/ppermute | solution.py:474
  344.8 39.3 %collective-permute-start.44 = (bf16[768,384]{1,0:T(8,128)(2,1)}, bf16[768,384]{1,0:T(8,128)(2,1)S(1)}, u32[]{:S(2)}, u32[]{:S(2)}) collective-permute-start(bf16[768,384]{1,0:T(8,128)(2,1)} %get-tuple-element.114), channel_id=1, source_target_pairs={{0,8},{4,12},{8,0},{12,4},{16,24},{20,28},{24,16},{28,20},{1,9},{5... | collective-permute-start | bytes 1769480 | tf_op jit(solution)/shard_map/ppermute | solution.py:474
  386.6 20.5 %collective-permute-start.52 = (bf16[200,384]{1,0:T(8,128)(2,1)S(1)}, bf16[200,384]{1,0:T(8,128)(2,1)S(1)}, u32[]{:S(2)}, u32[]{:S(2)}) collective-permute-start(bf16[200,384]{1,0:T(8,128)(2,1)S(1)} %get-tuple-element.186), channel_id=1, source_target_pairs={{0,3},{1,0},{2,1},{3,2},{4,7},{5,4},{6,5},{7,6},{8,11},{9,8},{10,9... | collective-permute-start | bytes 460808 | tf_op jit(solution)/shard_map/ppermute | solution.py:495
  386.7 28.6 %collective-permute-start.51 = (bf16[200,384]{1,0:T(8,128)(2,1)S(1)}, bf16[200,384]{1,0:T(8,128)(2,1)}, u32[]{:S(2)}, u32[]{:S(2)}) collective-permute-start(bf16[200,384]{1,0:T(8,128)(2,1)S(1)} %get-tuple-element.185), channel_id=1, source_target_pairs={{0,2},{1,3},{2,0},{3,1},{4,6},{5,7},{6,4},{7,5},{8,10},{9,11},{10,... | collective-permute-start | bytes 460808 | tf_op jit(solution)/shard_map/ppermute | solution.py:495
  403.3 14.7 %collective-permute-start.67 = (bf16[192,768]{1,0:T(8,128)(2,1)}, bf16[192,768]{1,0:T(8,128)(2,1)}, u32[]{:S(2)}, u32[]{:S(2)}) collective-permute-start(bf16[192,768]{1,0:T(8,128)(2,1)} %get-tuple-element.182), channel_id=1, source_target_pairs={{0,3},{1,0},{2,1},{3,2},{4,7},{5,4},{6,5},{7,6},{8,11},{9,8},{10,9... | collective-permute-start | bytes 884744 | tf_op jit(solution)/shard_map/ppermute | solution.py:495
  407.1 30.5 %collective-permute-start.66 = (bf16[192,768]{1,0:T(8,128)(2,1)}, bf16[192,768]{1,0:T(8,128)(2,1)}, u32[]{:S(2)}, u32[]{:S(2)}) collective-permute-start(bf16[192,768]{1,0:T(8,128)(2,1)} %get-tuple-element.183), channel_id=1, source_target_pairs={{0,2},{1,3},{2,0},{3,1},{4,6},{5,7},{6,4},{7,5},{8,10},{9,11},{10,... | collective-permute-start | bytes 884744 | tf_op jit(solution)/shard_map/ppermute | solution.py:495
  415.3 23.8 %collective-permute-start.65 = (bf16[192,768]{1,0:T(8,128)(2,1)}, bf16[192,768]{1,0:T(8,128)(2,1)}, u32[]{:S(2)}, u32[]{:S(2)}) collective-permute-start(bf16[192,768]{1,0:T(8,128)(2,1)} %get-tuple-element.181), channel_id=1, source_target_pairs={{0,1},{1,2},{2,3},{3,0},{4,5},{5,6},{6,7},{7,4},{8,9},{9,10},{10,1... | collective-permute-start | bytes 884744 | tf_op jit(solution)/shard_map/ppermute | solution.py:495
  416.5 26.0 %collective-permute-start.53 = (bf16[192,384]{1,0:T(8,128)(2,1)S(1)}, bf16[192,384]{1,0:T(8,128)(2,1)S(1)}, u32[]{:S(2)}, u32[]{:S(2)}) collective-permute-start(bf16[192,384]{1,0:T(8,128)(2,1)S(1)} %slice.269.refs_0_), channel_id=1, source_target_pairs={{0,8},{4,12},{8,0},{12,4},{16,24},{20,28},{24,16},{28,20},{1,9},{5... | collective-permute-start | bytes 442376 | tf_op jit(solution)/shard_map/ppermute | solution.py:474
  418.0 26.0 %collective-permute-start.54 = (bf16[192,384]{1,0:T(8,128)(2,1)S(1)}, bf16[192,384]{1,0:T(8,128)(2,1)S(1)}, u32[]{:S(2)}, u32[]{:S(2)}) collective-permute-start(bf16[192,384]{1,0:T(8,128)(2,1)S(1)} %slice.269.refs_0_), channel_id=1, source_target_pairs={{0,16},{4,20},{8,24},{12,28},{16,0},{20,4},{24,8},{28,12},{1,17},{... | collective-permute-start | bytes 442376 | tf_op jit(solution)/shard_map/ppermute | solution.py:474
  442.5 13.9 %collective-permute-start.70 = (bf16[192,768]{1,0:T(8,128)(2,1)S(1)}, bf16[192,768]{1,0:T(8,128)(2,1)}, u32[]{:S(2)}, u32[]{:S(2)}) collective-permute-start(bf16[192,768]{1,0:T(8,128)(2,1)S(1)} %fusion.26.refs_0_), channel_id=1, source_target_pairs={{0,24},{4,28},{8,16},{12,20},{16,8},{20,12},{24,0},{28,4},{1,25},{... | collective-permute-start | bytes 884744 | tf_op jit(solution)/shard_map/ppermute | solution.py:474
  445.9 29.8 %collective-permute-start.71 = (bf16[192,768]{1,0:T(8,128)(2,1)S(1)}, bf16[192,768]{1,0:T(8,128)(2,1)S(1)}, u32[]{:S(2)}, u32[]{:S(2)}) collective-permute-start(bf16[192,768]{1,0:T(8,128)(2,1)S(1)} %fusion.26.refs_0_), channel_id=1, source_target_pairs={{0,4},{4,0},{8,12},{12,8},{16,20},{20,16},{24,28},{28,24},{1,5},{5... | collective-permute-start | bytes 884744 | tf_op jit(solution)/shard_map/ppermute | solution.py:474
  451.3 25.3 %collective-permute-start.72 = (bf16[192,768]{1,0:T(8,128)(2,1)S(1)}, bf16[192,768]{1,0:T(8,128)(2,1)}, u32[]{:S(2)}, u32[]{:S(2)}) collective-permute-start(bf16[192,768]{1,0:T(8,128)(2,1)S(1)} %collective-permute-done.68.refs_1_), channel_id=1, source_target_pairs={{0,4},{4,0},{8,12},{12,8},{16,20},{20,16},{24,28},{28,24},{1,5},{5... | collective-permute-start | bytes 884744 | tf_op jit(solution)/shard_map/ppermute | solution.py:474
  454.9 22.7 %collective-permute-start.73 = (bf16[192,768]{1,0:T(8,128)(2,1)}, bf16[192,768]{1,0:T(8,128)(2,1)}, u32[]{:S(2)}, u32[]{:S(2)}) collective-permute-start(bf16[192,768]{1,0:T(8,128)(2,1)} %collective-permute-done.69.refs_2_), channel_id=1, source_target_pairs={{0,4},{4,0},{8,12},{12,8},{16,20},{20,16},{24,28},{28,24},{1,5},{5... | collective-permute-start | bytes 884744 | tf_op jit(solution)/shard_map/ppermute | solution.py:474
  456.4 21.2 %collective-permute-start.74 = (bf16[192,768]{1,0:T(8,128)(2,1)}, bf16[192,768]{1,0:T(8,128)(2,1)}, u32[]{:S(2)}, u32[]{:S(2)}) collective-permute-start(bf16[192,768]{1,0:T(8,128)(2,1)} %collective-permute-done.70.refs_3_), channel_id=1, source_target_pairs={{0,4},{4,0},{8,12},{12,8},{16,20},{20,16},{24,28},{28,24},{1,5},{5... | collective-permute-start | bytes 884744 | tf_op jit(solution)/shard_map/ppermute | solution.py:474
  466.1 44.7 %collective-permute-start.42 = (bf16[512,768]{1,0:T(8,128)(2,1)}, bf16[512,768]{1,0:T(8,128)(2,1)S(1)}, u32[]{:S(2)}, u32[]{:S(2)}) collective-permute-start(bf16[512,768]{1,0:T(8,128)(2,1)} %get-tuple-element.112), channel_id=1, source_target_pairs={{0,24},{4,28},{8,16},{12,20},{16,8},{20,12},{24,0},{28,4},{1,25},{... | collective-permute-start | bytes 2359304 | tf_op jit(solution)/shard_map/ppermute | solution.py:474
  475.7 35.1 %collective-permute-start.41 = (bf16[512,768]{1,0:T(8,128)(2,1)}, bf16[512,768]{1,0:T(8,128)(2,1)}, u32[]{:S(2)}, u32[]{:S(2)}) collective-permute-start(bf16[512,768]{1,0:T(8,128)(2,1)} %get-tuple-element.111), channel_id=1, source_target_pairs={{0,16},{4,20},{8,24},{12,28},{16,0},{20,4},{24,8},{28,12},{1,17},{... | collective-permute-start | bytes 2359304 | tf_op jit(solution)/shard_map/ppermute | solution.py:474
  476.5 34.3 %collective-permute-start.40 = (bf16[512,768]{1,0:T(8,128)(2,1)}, bf16[512,768]{1,0:T(8,128)(2,1)}, u32[]{:S(2)}, u32[]{:S(2)}) collective-permute-start(bf16[512,768]{1,0:T(8,128)(2,1)} %get-tuple-element.110), channel_id=1, source_target_pairs={{0,8},{4,12},{8,0},{12,4},{16,24},{20,28},{24,16},{28,20},{1,9},{5... | collective-permute-start | bytes 2359304 | tf_op jit(solution)/shard_map/ppermute | solution.py:474
  (108 other events, 1091.6 us)
